TPU v7x, 256 devices: a whole 4x4x8 slice. The times are simulated.
256 devices in a mesh: edges: 256 (over y, z, x, core).
Axes of the slice: x: 4, y: 4, z: 8, core: 2. Of those that a mesh axis runs over, the one named last changes fastest.
Arguments:
- messages: float32 [98304, 512], P('edges'), may hold values from -6 to 6
- rev_slot: int32 [98304], P('edges'), may hold values from 0 to 95
- tri_basis: float32 [16, 393216], P(None, 'edges'), may hold values from -6 to 6
- tri_source: int32 [393216], P('edges'), may hold values from 0 to 575
- tri_target: int32 [393216], P('edges'), may hold values from 0 to 127
- tile_block: int32 [3072], P('edges'), may hold values from 0 to 2
- tile_count: int32 [256], P('edges'), may hold values from 6 to 12, as said below
- w_basis: float32 [16, 512], replicated, may hold values from -1.5 to 1.5
- w_rev: float32 [512, 512], replicated, may hold values from -0.25 to 0.25
- w_layers: float32 [2, 512, 512], replicated, may hold values from -0.25 to 0.25
- cotangent: float32 [98304, 512], P('edges'), may hold values from -6 to 6
Outputs:
- out_messages: float32 [98304, 512], P('edges')
- grad_messages: float32 [98304, 512], P('edges')
- grad_layers: float32 [2, 262144], P(None, 'edges')
- grad_rev: float32 [262144], P('edges')
- grad_basis: float32 [16, 512], replicated
Inputs may be any that keep to these rules, and one draw needn't show every extreme that they name: Tiles j >= tile_count[d] of device d are ignored whatever they hold; some device has 12 live tiles.
All inputs are finite; a program needn't handle non-finite values.
Results may differ from a plain program's by a relative error of at most 0.0003.
Values sent between devices are 32-bit elements; how exact they have to be, the bound alone decides.
No kernel may reach another device: no remote copies, remote signals or barrier semaphores. Data moves between devices by JAX's collectives and lax.ppermute only.
A program may use at most 64 MiB of HBM per device.

v0:
```python
import jax
import jax.numpy as jnp
from jax import lax
from jax.experimental import pallas as pl
from jax.experimental.pallas import tpu as pltpu
from jax.sharding import PartitionSpec as P


F32, BF16, I32 = jnp.float32, jnp.bfloat16, jnp.int32
D, E, HALO, SLOTS, TILES = 512, 384, 96, 1536, 12
WIN = E + 2 * HALO
PAD = 640
HALF, PART = 768, 384
CHUNK = 512


def split(value):
    high = value.astype(BF16)
    return high, (value - high.astype(F32)).astype(BF16)


def nn(a, b):
    return lax.dot_general(a, b, (((1,), (0,)), ((), ())), preferred_element_type=F32)


def nt(a, b):
    return lax.dot_general(a, b, (((1,), (1,)), ((), ())), preferred_element_type=F32)


def tn(a, b):
    return lax.dot_general(a, b, (((0,), (0,)), ((), ())), preferred_element_type=F32)


def dot3(op, a, b):
    return op(a[0], b[0]) + (op(a[1], b[0]) + op(a[0], b[1]))


def onehot(values, base, lanes):
    shifted = (values - float(base)).astype(BF16)
    return jnp.where(shifted == lanes, jnp.ones_like(lanes), jnp.zeros_like(lanes))


def prepare(
    me, count, blocks, ints, coeffs, wb, m, core_in, side_in, wl,
    gath, tw, agg, ot, t2, r, rt, pick, wl_hi, wl_lo,
    ow, w2, tt, th, tl, c3, w3, wl_s, sem,
):
    copy = pltpu.make_async_copy(wl, wl_s, sem)
    copy.start()
    lane = lax.broadcasted_iota(I32, (128, 128), 1).astype(F32).astype(BF16)
    sub = lax.broadcasted_iota(I32, (128, 128), 0).astype(F32).astype(BF16)
    n_live = count[0]
    odd = me[0] & 1

    def tile(j, carry):
        start = pl.multiple_of(j * 128, 128)
        at = pl.ds(start, 128)
        w = ints[:, at]
        low = w + (E + HALO) - HALO * odd
        high = w - HALO * (1 - odd)
        u = jnp.where(w < HALO, low, jnp.where(w >= E + HALO, high, w - HALO))
        t = ints[:, pl.ds(pl.multiple_of(SLOTS + j * 128, 128), 128)] + blocks[j] * 128
        t = jnp.where(j < n_live, t, -1)
        ub = jnp.broadcast_to(u.astype(F32), (128, 128))
        tb = jnp.broadcast_to(t.astype(F32), (128, 128))
        for k in range(5):
            rows = 128 if k < 4 else 64
            ot[k * 128 : k * 128 + rows, at] = onehot(ub, k * 128, sub)[:rows]
        for k in range(3):
            tt[k * 128 : k * 128 + 128, at] = onehot(tb, k * 128, sub)
        uc = jnp.transpose(ub)
        tc = jnp.transpose(tb)
        for k in range(5):
            hit = onehot(uc, k * 128, lane)
            ow[at, k * 128 : k * 128 + 128] = hit
            ow[at, PAD + k * 128 : PAD + k * 128 + 128] = hit
        for k in range(3):
            hit = onehot(tc, k * 128, lane)
            t2[at, k * 128 : k * 128 + 128] = hit
            t2[at, E + k * 128 : E + k * 128 + 128] = hit
        return carry

    lax.fori_loop(0, TILES, tile, 0)
    position = lax.broadcasted_iota(I32, (1, E), 1)
    group = (position >= HALO).astype(I32) + (position >= 2 * HALO).astype(I32) + (position >= 3 * HALO).astype(I32)
    partner_row = (ints[:, 2 * SLOTS :] + group * HALO).astype(F32)
    for k in range(3):
        pb = jnp.broadcast_to(partner_row[:, k * 128 : k * 128 + 128], (128, 128))
        pc = jnp.transpose(pb)
        for i in range(3):
            rt[i * 128 : i * 128 + 128, k * 128 : k * 128 + 128] = onehot(pb, i * 128, sub)
            r[k * 128 : k * 128 + 128, i * 128 : i * 128 + 128] = onehot(pc, i * 128, lane)
    row = lax.broadcasted_iota(I32, (1, D), 1)
    j = jnp.bitwise_xor(row >> 1, me[0])
    bit = [(j >> b) & 1 for b in range(8)]
    order = [
        bit[0], bit[1] ^ bit[2], bit[2], bit[6] ^ bit[7], bit[7], bit[3], bit[4] ^ bit[5], bit[5], row & 1,
    ]
    place = order[0]
    for b in order[1:]:
        place = 2 * place + b
    hits = jnp.broadcast_to(place, (D, D)) == lax.broadcasted_iota(I32, (D, D), 0)
    pick[...] = jnp.where(hits, 1.0, 0.0).astype(BF16)
    for at, rows, source in ((0, E, m[...]), (E, HALO, core_in[HALO:, :]), (E + HALO, HALO, side_in[...])):
        w2[at : at + rows], w2[PAD + at : PAD + at + rows] = split(source)
    w2[WIN:PAD] = jnp.zeros((PAD - WIN, D), BF16)
    w2[PAD + WIN :] = jnp.zeros((PAD - WIN, D), BF16)
    high, low = split(coeffs[...])
    c3[:16], c3[16:32], c3[32:] = high, high, low
    high, low = split(wb[...])
    w3[:16], w3[16:32], w3[32:] = high, low, high

    for i in range(SLOTS // CHUNK):
        at = slice(i * CHUNK, (i + 1) * CHUNK)
        weight = tn(c3[:, at], w3[...])
        rows = nn(ow[at, :], w2[...])
        tw[at, :] = weight
        gath[at, :] = rows
        th[at, :], tl[at, :] = split(rows * weight)
    agg[...] = nn(tt[...], th[...]) + nn(tt[...], tl[...])
    copy.wait()
    for l in range(2):
        wl_hi[l], wl_lo[l] = split(wl_s[l])


def slope(v, s):
    return s * (1.0 + v * (1.0 - s))


def middle(
    core_in, a1, a2, a3, m, cot, gath, tw, agg, t2, r, rt, pick, coeffs, wr, wl_hi, wl_lo,
    out, gmp, gr0, gr1, gr2, gr3, wt_hi, wt_lo, own, send,
    wr_hi, wr_lo, g2, p, c_s, hs, gp_hi, gp_lo, left,
):
    scale = float(98304) ** -0.5
    arrived = jnp.concatenate([core_in[:HALO, :], a1[...], a2[...], a3[...]], axis=0)
    high, low = split(arrived)
    hs[2, :E] = nn(r[...], high).astype(BF16)
    hs[2, E:] = nn(r[...], low).astype(BF16)
    wr_hi[...], wr_lo[...] = split(wr[...])
    w_rev = (wr_hi[...], wr_lo[...])
    rp = dot3(nn, (hs[2, :E], hs[2, E:]), w_rev)
    left[2] = nt(pick[...], hs[2]).astype(BF16)
    rs = jax.nn.sigmoid(rp)
    gate = rp * rs
    h = m[...] + agg[...] + m[...] * gate
    pre, sig = [], []
    for l in range(2):
        hs[l, :E], hs[l, E:] = split(h)
        v = dot3(nn, (hs[l, :E], hs[l, E:]), (wl_hi[l], wl_lo[l]))
        left[l] = nt(pick[...], hs[l]).astype(BF16)
        s = jax.nn.sigmoid(v)
        pre.append(v)
        sig.append(s)
        h = h + v * s
    out[...] = h

    def weight_grad(k):
        gw = (nn(left[k], gp_hi[k]) + nn(left[k, :, :E], gp_lo[k])) * scale
        for half, ref in ((0, own), (256, send)):
            for part in range(4):
                first, last = max(part * PART, k * D), min(part * PART + PART, k * D + D)
                if first >= last:
                    continue
                if part == 0:
                    ref[:256, first:last] = gw[half : half + 256, first - k * D : last - k * D]
                    continue
                for block in range(16):
                    xa, xb, ya, yb = ((block >> b) & 1 for b in (3, 2, 1, 0))
                    to = ((xa, xb, ya, yb), (xb, xa, ya, yb), (ya, yb, xa, xb), (yb, ya, xa, xb))[part]
                    to = 16 * (8 * to[0] + 4 * to[1] + 2 * to[2] + to[3])
                    row = half + 16 * block
                    ref[to : to + 16, first:last] = gw[row : row + 16, first - k * D : last - k * D]

    g = cot[...]
    for l in (1, 0):
        high, low = split(g * slope(pre[l], sig[l]))
        gp_hi[l, :E], gp_hi[l, E:], gp_lo[l] = high, high, low
        g = g + dot3(nt, (gp_hi[l, :E], gp_lo[l]), (wl_hi[l], wl_lo[l]))
        weight_grad(l)
    g2[:E], g2[E:] = split(g)
    gmp[...] = g * (1.0 + gate)
    high, low = split(g * m[...] * slope(rp, rs))
    gp_hi[2, :E], gp_hi[2, E:], gp_lo[2] = high, high, low
    q = (nn(rt[...], gp_hi[2, :E]).astype(BF16), nn(rt[...], gp_lo[2]).astype(BF16))
    rows = dot3(nt, q, w_rev)
    for k, ref in enumerate((gr0, gr1, gr2, gr3)):
        ref[...] = rows[k * HALO : k * HALO + HALO]
    for i in range(SLOTS // CHUNK):
        at = slice(i * CHUNK, (i + 1) * CHUNK)
        prod = nn(t2[at, :], g2[...])
        p[0, at, :], p[1, at, :] = split(prod * gath[at, :])
        wt_hi[at, :], wt_lo[at, :] = split(prod * tw[at, :])
    weight_grad(2)
    c_s[:16], c_s[16:] = split(coeffs[...])
    both = nn(c_s[...], p[0])
    basis = (both[:16] + both[16:] + nn(c_s[:16], p[1])) * scale
    for ref in (own, send):
        ref[256:264, :512] = basis[:8]
        ref[256:264, 512:1024] = basis[8:]
        ref[256:264, 1024:] = jnp.zeros((8, 512), F32)


def scatter(ot, wt_hi, wt_lo, gmp, gr0, gm, core_out, side_out):
    rims = nn(ot[E:, :], wt_hi[...]) + nn(ot[E:, :], wt_lo[...])
    core_out[:HALO] = gr0[...]
    core_out[HALO:] = rims[:HALO]
    side_out[...] = rims[HALO:]
    gm[...] = gmp[...] + (nn(ot[:E, :], wt_hi[...]) + nn(ot[:E, :], wt_lo[...]))


def finish(me, gm, core_in, g1, g2, g3, side_in, out):
    odd = me[0] & 1
    out[:HALO] = gm[:HALO] + core_in[:HALO]
    for k, ref in enumerate((g1, g2, g3)):
        at = slice((k + 1) * HALO, (k + 2) * HALO)
        out[at] = gm[at] + ref[...]
    last = E - HALO
    at = pl.ds(pl.multiple_of(last * (1 - odd), 32), HALO)
    out[at, :] = out[at, :] + core_in[HALO:]
    at = pl.ds(pl.multiple_of(last * odd, 32), HALO)
    out[at, :] = out[at, :] + side_in[...]


def halves(rows, extra, keep, send):
    n = rows.shape[0] // 2
    keep[...] = rows[:n]
    send[:n] = rows[n:]
    send[n:] = extra


def fold_core(own, got, *refs):
    for part in range(4):
        at = slice(part * PART, (part + 1) * PART)
        halves(own[:256, at] + got[:256, at], own[256:, at] + got[256:, at], refs[2 * part], refs[2 * part + 1])


def fold_merge(keep_1, send_1, got_1, keep_2, send_2, got_2, keep_next, send_next):
    n = keep_1.shape[0]
    for at, keep, send, got in ((slice(0, PART), keep_1, send_1, got_1), (slice(PART, HALF), keep_2, send_2, got_2)):
        rows = keep[...] + got[:n]
        keep_next[:, at] = rows[: n // 2]
        send_next[: n // 2, at] = rows[n // 2 :]
        send_next[n // 2 :, at] = send[n:] + got[n:]


def fold(keep, send, got, keep_next, send_next):
    n = keep.shape[0]
    halves(keep[...] + got[:n], send[n:] + got[n:], keep_next, send_next)


def fold_join(keep_a, send_a, got_a, keep_b, send_b, got_b, keep_next, send_1, send_2, send_3):
    n = keep_a.shape[0]
    for at, keep, send, got in ((slice(0, HALF), keep_a, send_a, got_a), (slice(HALF, 2 * HALF), keep_b, send_b, got_b)):
        rows = keep[...] + got[:n]
        extra = send[n:] + got[n:]
        keep_next[:, at] = rows[:4]
        for k, ref in ((8, send_1), (4, send_2), (12, send_3)):
            ref[:4, at] = rows[k : k + 4]
            ref[4:, at] = extra


def fold_four(keep, send, got_1, got_2, got_3, keep_next, send_next):
    rows = (keep[...] + got_2[:4]) + (got_1[:4] + got_3[:4])
    extra = (send[4:] + got_2[4:]) + (got_1[4:] + got_3[4:])
    halves(rows, extra, keep_next, send_next)


def fold_last(keep, send, got, layers, rev, basis):
    rows = keep[...] + got[:2]
    extra = send[2:] + got[2:]
    for k in range(3):
        for a in range(2):
            piece = rows[a : a + 1, k * D : k * D + D]
            if k < 2:
                layers[k : k + 1, a * D : a * D + D] = piece
            else:
                rev[:, a * D : a * D + D] = piece
    basis[:8] = extra[:, :D]
    basis[8:] = extra[:, D : 2 * D]


def call(kernel, outs, specs, scratch=(), flops=1_000_000, grant=8):
    places = {
        "s": pl.BlockSpec(memory_space=pltpu.SMEM),
        "v": pl.BlockSpec(memory_space=pltpu.VMEM),
        "h": pl.BlockSpec(memory_space=pltpu.HBM),
    }
    return pl.pallas_call(
        kernel,
        out_shape=[jax.ShapeDtypeStruct(shape, dtype) for shape, dtype in outs],
        in_specs=[places[c] for c in specs],
        out_specs=[places["v"]] * len(outs),
        scratch_shapes=list(scratch),
        compiler_params=pltpu.CompilerParams(vmem_limit_bytes=grant << 20),
        cost_estimate=pl.CostEstimate(flops=flops, bytes_accessed=1 << 20, transcendentals=0),
    )


def swap(value, mask):
    count = lax.axis_size("edges")
    return lax.ppermute(value, "edges", [(i, i ^ mask) for i in range(count)])


def swap_side(value):
    count = lax.axis_size("edges")
    return lax.ppermute(value, "edges", [(i, (i + (1 if i % 2 else -1)) % count) for i in range(count)])


def tie(value, *others):
    return lax.optimization_barrier((value, *others))[0]


def step(state, got):
    keep, send = state
    n, columns = keep.shape
    return call(fold, [((n // 2, columns), F32), ((n // 2 + 8, columns), F32)], "vvv")(keep, send, got)


def on_device_body(messages, rev_slot, tri_basis, tri_source, tri_target, tile_block, tile_count, w_basis, w_rev, w_layers, cotangent):
    index = lax.axis_index("edges").astype(I32)
    me = index.reshape(1)
    odd = index & 1
    quarter = ((HALO, D), F32)
    toward_core = lax.dynamic_slice_in_dim(messages, (E - HALO) * (1 - odd), HALO)
    toward_side = lax.dynamic_slice_in_dim(messages, (E - HALO) * odd, HALO)
    a2 = swap(messages[2 * HALO : 3 * HALO], 32)
    side_in = swap_side(toward_side)
    core_in = swap(jnp.concatenate([messages[:HALO], toward_core], axis=0), 1)
    a3 = swap(messages[3 * HALO :], 128)
    a1 = swap(messages[HALO : 2 * HALO], 4)
    ints = jnp.concatenate([tri_source, tri_target, rev_slot]).reshape(1, 2 * SLOTS + E)
    (gath, tw, agg, ot, t2, r, rt, pick, wl_hi, wl_lo) = call(
        prepare,
        [
            ((SLOTS, D), F32), ((SLOTS, D), F32), ((E, D), F32), ((WIN, SLOTS), BF16), ((SLOTS, 2 * E), BF16),
            ((E, E), BF16), ((E, E), BF16), ((D, D), BF16),
            ((2, D, D), BF16), ((2, D, D), BF16),
        ],
        "sss" + "v" * 6 + "h",
        [
            pltpu.VMEM((SLOTS, 2 * PAD), BF16), pltpu.VMEM((2 * PAD, D), BF16), pltpu.VMEM((E, SLOTS), BF16),
            pltpu.VMEM((SLOTS, D), BF16), pltpu.VMEM((SLOTS, D), BF16),
            pltpu.VMEM((48, SLOTS), BF16), pltpu.VMEM((48, D), BF16),
            pltpu.VMEM((2, D, D), F32), pltpu.SemaphoreType.DMA,
        ],
        flops=4_000_000_000,
        grant=26,
    )(me, tile_count, tile_block, ints, tri_basis, w_basis, messages, core_in, side_in, w_layers)
    out, gmp, gr0, gr1, gr2, gr3, wt_hi, wt_lo, own, send = call(
        middle,
        [
            ((E, D), F32), ((E, D), F32), quarter, quarter, quarter, quarter,
            ((SLOTS, D), BF16), ((SLOTS, D), BF16), ((264, 3 * D), F32), ((264, 3 * D), F32),
        ],
        "v" * 17,
        [
            pltpu.VMEM((D, D), BF16), pltpu.VMEM((D, D), BF16),
            pltpu.VMEM((2 * E, D), BF16), pltpu.VMEM((2, SLOTS, D), BF16), pltpu.VMEM((32, SLOTS), BF16),
            pltpu.VMEM((3, 2 * E, D), BF16), pltpu.VMEM((3, 2 * E, D), BF16), pltpu.VMEM((3, E, D), BF16),
            pltpu.VMEM((3, D, 2 * E), BF16),
        ],
        flops=16_000_000_000,
        grant=16,
    )(core_in, a1, a2, a3, messages, cotangent, gath, tw, agg, t2, r, rt, pick, tri_basis, w_rev, wl_hi, wl_lo)

    got = swap(send, 1)
    b2 = swap(gr2, 32)
    gm, core_out, side_out = call(
        scatter, [((E, D), F32), ((2 * HALO, D), F32), quarter], "v" * 5, flops=1_000_000_000, grant=6
    )(ot, wt_hi, wt_lo, gmp, gr0)
    core_back = swap(core_out, 1)
    side_back = swap_side(side_out)
    b1 = swap(gr1, 4)
    b3 = swap(gr3, 128)
    (grad_messages,) = call(finish, [((E, D), F32)], "s" + "v" * 6)(me, gm, core_back, b1, b2, b3, side_back)
    parts = call(fold_core, [((128, PART), F32), ((136, PART), F32)] * 4, "vv")(own, got)
    parts = [parts[2 * k : 2 * k + 2] for k in range(4)]
    gots = [swap(part[1], mask) for part, mask in zip(parts, (2, 6, 64, 192))]
    parts = [step(part, arrived) for part, arrived in zip(parts, gots)]
    gots = [swap(part[1], mask) for part, mask in zip(parts, (6, 2, 192, 64))]
    a, b = (
        call(fold_merge, [((32, HALF), F32), ((40, HALF), F32)], "v" * 6)(
            *parts[k], gots[k], *parts[k + 1], gots[k + 1]
        )
        for k in (0, 2)
    )
    got_a, got_b = swap(a[1], 64), swap(b[1], 2)
    a, b = step(a, got_a), step(b, got_b)
    got_a, got_b = swap(a[1], 192), swap(b[1], 6)
    keep, send_1, send_2, send_3 = call(fold_join, [((4, 3 * D), F32)] + [((12, 3 * D), F32)] * 3, "v" * 6)(
        *a, got_a, *b, got_b
    )
    got_1, got_2, got_3 = swap(send_1, 8), swap(send_2, 16), swap(send_3, 24)
    c = call(fold_four, [((2, 3 * D), F32), ((10, 3 * D), F32)], "v" * 5)(keep, send_1, got_1, got_2, got_3)
    got = tie(swap(c[1], 48), grad_messages)
    layers, rev, basis = call(fold_last, [((2, 2 * D), F32), ((1, 2 * D), F32), ((16, D), F32)], "vvv")(*c, got)
    return (out, grad_messages, layers, rev.reshape(2 * D), basis)


def solution(mesh):
    split_rows, flat = P("edges", None), P("edges")
    in_specs = (split_rows, flat, P(None, "edges"), flat, flat, flat, flat, P(), P(), P(), split_rows)
    out_specs = (split_rows, split_rows, P(None, "edges"), flat, P())
    return jax.shard_map(on_device_body, mesh=mesh, in_specs=in_specs, out_specs=out_specs, check_vma=False)
```

profile of v0, /device:TPU:1, one launch (start us, length us, event | category | flops | bytes accessed | tf_op | source)
XLA Modules:
  0.0 102.0 jit_solution(8618346610073790114)
XLA Ops:
  0.7 1.6 %constant_dynamic-slice_fusion = (f32[96,512]{1,0:T(8,128)S(1)}, f32[96,512]{1,0:T(8,128)S(1)}, f32[96,512]{1,0:T(8,128)S(1)}, f32[96,512]{1,0:T(8,128)S(1)}, f32[96,512]{1,0:T(8,128)S(1)}, /*index=5*/f32[96,512]{1,0:T(8,128)S(1)}) fusion(f32[384,512]{1,0:T(8,128)} %m.3, s32[]{:T(128)S(6)} %select_n.7, s32[]{:T(128)S(6)} %select_n.6), kind=kLoop, calls=%fused_computation.2 | loop fusion | bytes 2359304 | tf_op jit(solution)/shard_map/dynamic_slice | solution.py:326
  2.4 3.3 %collective-permute-start = (f32[192,512]{1,0:T(8,128)S(1)}, f32[192,512]{1,0:T(8,128)S(1)}, u32[]{:S(2)}, u32[]{:S(2)}) collective-permute-start(f32[192,512]{1,0:T(8,128)S(1)} %pad_maximum_fusion), channel_id=1, source_target_pairs={{0,1},{1,0},{2,3},{3,2},{4,5},{5,4},{6,7},{7,6},{8,9},{9,8},{10,11... | collective-permute-start | bytes 1179656 | tf_op jit(solution)/shard_map/ppermute | solution.py:302
  5.6 2.4 %collective-permute-start.3 = (f32[96,512]{1,0:T(8,128)S(1)}, f32[96,512]{1,0:T(8,128)S(1)}, u32[]{:S(2)}, u32[]{:S(2)}) collective-permute-start(f32[96,512]{1,0:T(8,128)S(1)} %get-tuple-element.120), channel_id=1, source_target_pairs={{0,128},{1,129},{2,130},{3,131},{4,132},{5,133},{6,134},{7,135},{8... | collective-permute-start | bytes 589832 | tf_op jit(solution)/shard_map/ppermute | solution.py:302
  8.0 6.9 %collective-permute-start.2 = (f32[96,512]{1,0:T(8,128)S(1)}, f32[96,512]{1,0:T(8,128)S(1)}, u32[]{:S(2)}, u32[]{:S(2)}) collective-permute-start(f32[96,512]{1,0:T(8,128)S(1)} %get-tuple-element.121), channel_id=1, source_target_pairs={{0,32},{1,33},{2,34},{3,35},{4,36},{5,37},{6,38},{7,39},{8,40},{9,... | collective-permute-start | bytes 589832 | tf_op jit(solution)/shard_map/ppermute | solution.py:302
  15.0 2.5 %collective-permute-start.1 = (f32[96,512]{1,0:T(8,128)S(1)}, f32[96,512]{1,0:T(8,128)S(1)}, u32[]{:S(2)}, u32[]{:S(2)}) collective-permute-start(f32[96,512]{1,0:T(8,128)S(1)} %get-tuple-element.122), channel_id=1, source_target_pairs={{0,4},{1,5},{2,6},{3,7},{4,0},{5,1},{6,2},{7,3},{8,12},{9,13},{10,... | collective-permute-start | bytes 589832 | tf_op jit(solution)/shard_map/ppermute | solution.py:302
  18.1 0.0 collective-permute-done.core_in
  18.2 0.0 copy-start.2
  18.2 0.0 copy-start.3
  18.2 7.1 %shard_map.146 = (f32[1536,512]{1,0:T(8,128)S(1)}, f32[1536,512]{1,0:T(8,128)S(1)}, f32[384,512]{1,0:T(8,128)S(1)}, bf16[576,1536]{1,0:T(8,128)(2,1)S(1)}, bf16[...) custom-call(s32[1]{0:T(128)} %bitcast.me, ...), custom_call_target="tpu_custom_call" | custom-call | flops 4000000000 | bytes 1048576 | tf_op jit(solution)/shard_map/pallas_call | solution.py:333
  25.4 0.0 collective-permute-done.3.a3
  25.4 10.4 %shard_map.147 = (f32[384,512]{1,0:T(8,128)}, f32[384,512]{1,0:T(8,128)S(1)}, f32[96,512]{1,0:T(8,128)S(1)}, f32[96,512]{1,0:T(8,128)S(1)}, f32[96,512]{1,0:T(8,...) custom-call(f32[192,512]{1,0:T(8,128)S(1)} %collective-permute-done., ...), custom_call_target="tpu_custom_call" | custom-call | flops 16000000000 | bytes 1048576 | tf_op jit(solution)/shard_map/pallas_call | solution.py:350
  35.8 8.0 %collective-permute-start.10 = (f32[264,1536]{1,0:T(8,128)S(1)}, f32[264,1536]{1,0:T(8,128)S(1)}, u32[]{:S(2)}, u32[]{:S(2)}) collective-permute-start(f32[264,1536]{1,0:T(8,128)S(1)} %get-tuple-element.84), channel_id=1, source_target_pairs={{0,1},{1,0},{2,3},{3,2},{4,5},{5,4},{6,7},{7,6},{8,9},{9,8},{10,11... | collective-permute-start | bytes 4866056 | tf_op jit(solution)/shard_map/ppermute | solution.py:302
  43.8 3.1 %collective-permute-done.10.got = f32[264,1536]{1,0:T(8,128)S(1)} collective-permute-done((f32[264,1536]{1,0:T(8,128)S(1)}, f32[264,1536]{1,0:T(8,128)S(1)}, u32[]{:S(2)}, u32[]{:S(2)}) %collective-permute-start.10) | collective-permute-done | bytes 1622048 | tf_op jit(solution)/shard_map/ppermute | solution.py:302
  46.9 0.2 shard_map.150
  47.1 0.1 collective-permute-start.11
  47.2 0.1 collective-permute-start.13
  47.3 0.1 collective-permute-start.17
  47.4 0.6 collective-permute-start.19
  48.0 5.5 %collective-permute-done.11.got = f32[136,384]{1,0:T(8,128)S(1)} collective-permute-done((f32[136,384]{1,0:T(8,128)S(1)}, f32[136,384]{1,0:T(8,128)S(1)}, u32[]{:S(2)}, u32[]{:S(2)}) %collective-permute-start.11) | collective-permute-done | bytes 208928 | tf_op jit(solution)/shard_map/ppermute | solution.py:302
  53.6 0.1 collective-permute-start.12
  53.7 1.2 %collective-permute-done.13.got = f32[136,384]{1,0:T(8,128)S(1)} collective-permute-done((f32[136,384]{1,0:T(8,128)S(1)}, f32[136,384]{1,0:T(8,128)S(1)}, u32[]{:S(2)}, u32[]{:S(2)}) %collective-permute-start.13) | collective-permute-done | bytes 208928 | tf_op jit(solution)/shard_map/ppermute | solution.py:302
  54.9 0.1 collective-permute-start.14
  55.0 0.6 collective-permute-start.18
  55.6 0.1 collective-permute-start.20
  55.7 2.7 %collective-permute-done.12.got_1 = f32[72,384]{1,0:T(8,128)S(1)} collective-permute-done((f32[72,384]{1,0:T(8,128)S(1)}, f32[72,384]{1,0:T(8,128)S(1)}, u32[]{:S(2)}, u32[]{:S(2)}) %collective-permute-start.12) | collective-permute-done | bytes 110624 | tf_op jit(solution)/shard_map/ppermute | solution.py:302
  58.5 0.1 collective-permute-done.14.got_2
  58.6 0.1 collective-permute-start.15
  58.7 1.5 %collective-permute-done.18.got_1 = f32[72,384]{1,0:T(8,128)S(1)} collective-permute-done((f32[72,384]{1,0:T(8,128)S(1)}, f32[72,384]{1,0:T(8,128)S(1)}, u32[]{:S(2)}, u32[]{:S(2)}) %collective-permute-start.18) | collective-permute-done | bytes 110624 | tf_op jit(solution)/shard_map/ppermute | solution.py:302
  60.3 1.2 %collective-permute-start.21 = (f32[40,768]{1,0:T(8,128)S(1)}, f32[40,768]{1,0:T(8,128)S(1)}, u32[]{:S(2)}, u32[]{:S(2)}) collective-permute-start(f32[40,768]{1,0:T(8,128)S(1)} %get-tuple-element.106.send), channel_id=1, source_target_pairs={{0,2},{1,3},{2,0},{3,1},{4,6},{5,7},{6,4},{7,5},{8,10},{9,11},{10,... | collective-permute-start | bytes 368648 | tf_op jit(solution)/shard_map/ppermute | solution.py:302
  61.5 2.0 %shard_map.148 = (f32[384,512]{1,0:T(8,128)S(1)}, f32[192,512]{1,0:T(8,128)S(1)}, f32[96,512]{1,0:T(8,128)S(1)}) custom-call(bf16[576,1536]{1,0:T(8,128)(2,1)S(1)} %get-tuple-element.72.ot, bf16[1536,512]{1,0:T(8,128)(2,1)S(1)} %get-tuple-element.73.wt_hi, bf16[1536,512]{1,0:T(8,128)(2,1)S(1)} %get-tuple-element.74.wt_lo, ...), custom_call_target="tpu_custom_call" | custom-call | flops 1000000000 | bytes 1048576 | tf_op jit(solution)/shard_map/pallas_call | solution.py:369
  63.5 3.6 %collective-permute-start.5 = (f32[192,512]{1,0:T(8,128)S(1)}, f32[192,512]{1,0:T(8,128)S(1)}, u32[]{:S(2)}, u32[]{:S(2)}) collective-permute-start(f32[192,512]{1,0:T(8,128)S(1)} %get-tuple-element.78), channel_id=1, source_target_pairs={{0,1},{1,0},{2,3},{3,2},{4,5},{5,4},{6,7},{7,6},{8,9},{9,8},{10,11... | collective-permute-start | bytes 1179656 | tf_op jit(solution)/shard_map/ppermute | solution.py:302
  67.1 1.6 %collective-permute-start.16 = (f32[24,768]{1,0:T(8,128)S(1)}, f32[24,768]{1,0:T(8,128)S(1)}, u32[]{:S(2)}, u32[]{:S(2)}) collective-permute-start(f32[24,768]{1,0:T(8,128)S(1)} %get-tuple-element.96.send_a), channel_id=1, source_target_pairs={{0,192},{1,193},{2,194},{3,195},{4,196},{5,197},{6,198},{7,199},{8... | collective-permute-start | bytes 221192 | tf_op jit(solution)/shard_map/ppermute | solution.py:302
  68.8 1.6 %collective-permute-start.22 = (f32[24,768]{1,0:T(8,128)S(1)}, f32[24,768]{1,0:T(8,128)S(1)}, u32[]{:S(2)}, u32[]{:S(2)}) collective-permute-start(f32[24,768]{1,0:T(8,128)S(1)} %get-tuple-element.108.send_b), channel_id=1, source_target_pairs={{0,6},{1,7},{2,4},{3,5},{4,2},{5,3},{6,0},{7,1},{8,14},{9,15},{10,... | collective-permute-start | bytes 221192 | tf_op jit(solution)/shard_map/ppermute | solution.py:302
  70.4 1.8 %collective-permute-done.16.got_a = f32[24,768]{1,0:T(8,128)S(1)} collective-permute-done((f32[24,768]{1,0:T(8,128)S(1)}, f32[24,768]{1,0:T(8,128)S(1)}, u32[]{:S(2)}, u32[]{:S(2)}) %collective-permute-start.16) | collective-permute-done | bytes 73760 | tf_op jit(solution)/shard_map/ppermute | solution.py:302
  72.2 1.4 %collective-permute-done.22.got_b = f32[24,768]{1,0:T(8,128)S(1)} collective-permute-done((f32[24,768]{1,0:T(8,128)S(1)}, f32[24,768]{1,0:T(8,128)S(1)}, u32[]{:S(2)}, u32[]{:S(2)}) %collective-permute-start.22) | collective-permute-done | bytes 73760 | tf_op jit(solution)/shard_map/ppermute | solution.py:302
  73.6 0.1 collective-permute-start.24
  73.7 0.1 collective-permute-start.25
  73.8 2.5 %collective-permute-start.23 = (f32[12,1536]{1,0:T(8,128)S(1)}, f32[12,1536]{1,0:T(8,128)S(1)}, u32[]{:S(2)}, u32[]{:S(2)}) collective-permute-start(f32[12,1536]{1,0:T(8,128)S(1)} %get-tuple-element.110.send), channel_id=1, source_target_pairs={{0,8},{1,9},{2,10},{3,11},{4,12},{5,13},{6,14},{7,15},{8,0},{9,1},... | collective-permute-start | bytes 221192 | tf_op jit(solution)/shard_map/ppermute | solution.py:302
  76.3 1.2 %collective-permute-start.9 = (f32[96,512]{1,0:T(8,128)S(1)}, f32[96,512]{1,0:T(8,128)S(1)}, u32[]{:S(2)}, u32[]{:S(2)}) collective-permute-start(f32[96,512]{1,0:T(8,128)S(1)} %get-tuple-element.82), channel_id=1, source_target_pairs={{0,255},{1,2},{2,1},{3,4},{4,3},{5,6},{6,5},{7,8},{8,7},{9,10},{10... | collective-permute-start | bytes 589832 | tf_op jit(solution)/shard_map/ppermute | solution.py:307
  77.5 0.6 collective-permute-done.24.got_2
  78.2 2.8 %collective-permute-start.6 = (f32[96,512]{1,0:T(8,128)S(1)}, f32[96,512]{1,0:T(8,128)S(1)}, u32[]{:S(2)}, u32[]{:S(2)}) collective-permute-start(f32[96,512]{1,0:T(8,128)S(1)} %get-tuple-element.79), channel_id=1, source_target_pairs={{0,4},{1,5},{2,6},{3,7},{4,0},{5,1},{6,2},{7,3},{8,12},{9,13},{10,... | collective-permute-start | bytes 589832 | tf_op jit(solution)/shard_map/ppermute | solution.py:302
  80.9 4.9 %collective-permute-start.7 = (f32[96,512]{1,0:T(8,128)S(1)}, f32[96,512]{1,0:T(8,128)S(1)}, u32[]{:S(2)}, u32[]{:S(2)}) collective-permute-start(f32[96,512]{1,0:T(8,128)S(1)} %get-tuple-element.80), channel_id=1, source_target_pairs={{0,32},{1,33},{2,34},{3,35},{4,36},{5,37},{6,38},{7,39},{8,40},{9,... | collective-permute-start | bytes 589832 | tf_op jit(solution)/shard_map/ppermute | solution.py:302
  85.8 1.6 %collective-permute-start.8 = (f32[96,512]{1,0:T(8,128)S(1)}, f32[96,512]{1,0:T(8,128)S(1)}, u32[]{:S(2)}, u32[]{:S(2)}) collective-permute-start(f32[96,512]{1,0:T(8,128)S(1)} %get-tuple-element.81), channel_id=1, source_target_pairs={{0,128},{1,129},{2,130},{3,131},{4,132},{5,133},{6,134},{7,135},{8... | collective-permute-start | bytes 589832 | tf_op jit(solution)/shard_map/ppermute | solution.py:302
  87.5 3.7 %collective-permute-start.26 = (f32[10,1536]{1,0:T(8,128)S(1)}, f32[10,1536]{1,0:T(8,128)S(1)}, u32[]{:S(2)}, u32[]{:S(2)}) collective-permute-start(f32[10,1536]{1,0:T(8,128)S(1)} %get-tuple-element.114.send), channel_id=1, source_target_pairs={{0,48},{1,49},{2,50},{3,51},{4,52},{5,53},{6,54},{7,55},{8,56},{9,... | collective-permute-start | bytes 184328 | tf_op jit(solution)/shard_map/ppermute | solution.py:302
  91.2 1.0 collective-permute-done.8.g3
  92.2 1.0 shard_map.149
  93.2 8.1 %collective-permute-done.26.got = f32[10,1536]{1,0:T(8,128)S(1)} collective-permute-done((f32[10,1536]{1,0:T(8,128)S(1)}, f32[10,1536]{1,0:T(8,128)S(1)}, u32[]{:S(2)}, u32[]{:S(2)}) %collective-permute-start.26) | collective-permute-done | bytes 61472 | tf_op jit(solution)/shard_map/ppermute | solution.py:302
  101.3 0.6 shard_map.161
  (46 shorter events, 0.4 us)
Async XLA Ops:
  0.6 17.5 %copy-start = (f32[384,512]{1,0:T(8,128)S(1)}, f32[384,512]{1,0:T(8,128)}, u32[]{:S(2)}) copy-start(f32[384,512]{1,0:T(8,128)} %m.3) | copy-start | bytes 2359300
  0.6 17.4 %copy-start.7 = (s32[1536]{0:T(1024)S(1)}, s32[1536]{0:T(1024)}, u32[]{:S(2)}) copy-start(s32[1536]{0:T(1024)} %param.15) | copy-start | bytes 18436
  0.7 17.4 %copy-start.8 = (s32[1536]{0:T(1024)S(1)}, s32[1536]{0:T(1024)}, u32[]{:S(2)}) copy-start(s32[1536]{0:T(1024)} %param.14) | copy-start | bytes 18436
  0.7 17.4 %copy-start.9 = (s32[384]{0:T(512)S(1)}, s32[384]{0:T(512)}, u32[]{:S(2)}) copy-start(s32[384]{0:T(512)} %param.12) | copy-start | bytes 4612
  0.7 17.5 %copy-start.4 = (f32[16,1536]{1,0:T(8,128)S(1)}, f32[16,1536]{1,0:T(8,128)}, u32[]{:S(2)}) copy-start(f32[16,1536]{1,0:T(8,128)} %coeffs.3) | copy-start | bytes 294916
  0.7 17.5 %copy-start.1 = (f32[2,512,512]{2,1,0:T(8,128)S(1)}, f32[2,512,512]{2,1,0:T(8,128)}, u32[]{:S(2)}) copy-start(f32[2,512,512]{2,1,0:T(8,128)} %wl.1) | copy-start | bytes 6291460
  0.7 17.5 %copy-start.5 = (f32[16,512]{1,0:T(8,128)S(1)}, f32[16,512]{1,0:T(8,128)}, u32[]{:S(2)}) copy-start(f32[16,512]{1,0:T(8,128)} %wb.1) | copy-start | bytes 98308
  0.7 17.5 %copy-start.6 = (s32[12]{0:T(128)S(1)}, s32[12]{0:T(128)}, u32[]{:S(2)}) copy-start(s32[12]{0:T(128)} %blocks.1) | copy-start | bytes 148
  2.4 15.8 %collective-permute-start = (f32[192,512]{1,0:T(8,128)S(1)}, f32[192,512]{1,0:T(8,128)S(1)}, u32[]{:S(2)}, u32[]{:S(2)}) collective-permute-start(f32[192,512]{1,0:T(8,128)S(1)} %pad_maximum_fusion), channel_id=1, source_target_pairs={{0,1},{1,0},{2,3},{3,2},{4,5},{5,4},{6,7},{7,6},{8,9},{9,8},{10,11... | collective-permute-start | bytes 1179656 | tf_op jit(solution)/shard_map/ppermute | solution.py:302
  5.6 12.5 %collective-permute-start.4 = (f32[96,512]{1,0:T(8,128)S(1)}, f32[96,512]{1,0:T(8,128)S(1)}, u32[]{:S(2)}, u32[]{:S(2)}) collective-permute-start(f32[96,512]{1,0:T(8,128)S(1)} %get-tuple-element.119), channel_id=1, source_target_pairs={{0,255},{1,2},{2,1},{3,4},{4,3},{5,6},{6,5},{7,8},{8,7},{9,10},{10... | collective-permute-start | bytes 589832 | tf_op jit(solution)/shard_map/ppermute | solution.py:307
  5.6 19.7 %collective-permute-start.3 = (f32[96,512]{1,0:T(8,128)S(1)}, f32[96,512]{1,0:T(8,128)S(1)}, u32[]{:S(2)}, u32[]{:S(2)}) collective-permute-start(f32[96,512]{1,0:T(8,128)S(1)} %get-tuple-element.120), channel_id=1, source_target_pairs={{0,128},{1,129},{2,130},{3,131},{4,132},{5,133},{6,134},{7,135},{8... | collective-permute-start | bytes 589832 | tf_op jit(solution)/shard_map/ppermute | solution.py:302
  8.0 17.3 %collective-permute-start.2 = (f32[96,512]{1,0:T(8,128)S(1)}, f32[96,512]{1,0:T(8,128)S(1)}, u32[]{:S(2)}, u32[]{:S(2)}) collective-permute-start(f32[96,512]{1,0:T(8,128)S(1)} %get-tuple-element.121), channel_id=1, source_target_pairs={{0,32},{1,33},{2,34},{3,35},{4,36},{5,37},{6,38},{7,39},{8,40},{9,... | collective-permute-start | bytes 589832 | tf_op jit(solution)/shard_map/ppermute | solution.py:302
  15.0 10.4 %collective-permute-start.1 = (f32[96,512]{1,0:T(8,128)S(1)}, f32[96,512]{1,0:T(8,128)S(1)}, u32[]{:S(2)}, u32[]{:S(2)}) collective-permute-start(f32[96,512]{1,0:T(8,128)S(1)} %get-tuple-element.122), channel_id=1, source_target_pairs={{0,4},{1,5},{2,6},{3,7},{4,0},{5,1},{6,2},{7,3},{8,12},{9,13},{10,... | collective-permute-start | bytes 589832 | tf_op jit(solution)/shard_map/ppermute | solution.py:302
  18.2 7.2 %copy-start.2 = (f32[512,512]{1,0:T(8,128)S(1)}, f32[512,512]{1,0:T(8,128)}, u32[]{:S(2)}) copy-start(f32[512,512]{1,0:T(8,128)} %wr.1) | copy-start | bytes 3145732
  18.2 7.2 %copy-start.3 = (f32[384,512]{1,0:T(8,128)S(1)}, f32[384,512]{1,0:T(8,128)}, u32[]{:S(2)}) copy-start(f32[384,512]{1,0:T(8,128)} %cot.1) | copy-start | bytes 2359300
  35.8 11.1 %collective-permute-start.10 = (f32[264,1536]{1,0:T(8,128)S(1)}, f32[264,1536]{1,0:T(8,128)S(1)}, u32[]{:S(2)}, u32[]{:S(2)}) collective-permute-start(f32[264,1536]{1,0:T(8,128)S(1)} %get-tuple-element.84), channel_id=1, source_target_pairs={{0,1},{1,0},{2,3},{3,2},{4,5},{5,4},{6,7},{7,6},{8,9},{9,8},{10,11... | collective-permute-start | bytes 4866056 | tf_op jit(solution)/shard_map/ppermute | solution.py:302
  47.1 6.4 %collective-permute-start.11 = (f32[136,384]{1,0:T(8,128)S(1)}, f32[136,384]{1,0:T(8,128)S(1)}, u32[]{:S(2)}, u32[]{:S(2)}) collective-permute-start(f32[136,384]{1,0:T(8,128)S(1)} %get-tuple-element.86.send), channel_id=1, source_target_pairs={{0,2},{1,3},{2,0},{3,1},{4,6},{5,7},{6,4},{7,5},{8,10},{9,11},{10,... | collective-permute-start | bytes 626696 | tf_op jit(solution)/shard_map/ppermute | solution.py:302
  47.2 7.6 %collective-permute-start.13 = (f32[136,384]{1,0:T(8,128)S(1)}, f32[136,384]{1,0:T(8,128)S(1)}, u32[]{:S(2)}, u32[]{:S(2)}) collective-permute-start(f32[136,384]{1,0:T(8,128)S(1)} %get-tuple-element.90.send), channel_id=1, source_target_pairs={{0,6},{1,7},{2,4},{3,5},{4,2},{5,3},{6,0},{7,1},{8,14},{9,15},{10,... | collective-permute-start | bytes 626696 | tf_op jit(solution)/shard_map/ppermute | solution.py:302
  47.3 7.7 %collective-permute-start.17 = (f32[136,384]{1,0:T(8,128)S(1)}, f32[136,384]{1,0:T(8,128)S(1)}, u32[]{:S(2)}, u32[]{:S(2)}) collective-permute-start(f32[136,384]{1,0:T(8,128)S(1)} %get-tuple-element.98.send), channel_id=1, source_target_pairs={{0,64},{1,65},{2,66},{3,67},{4,68},{5,69},{6,70},{7,71},{8,72},{9,... | collective-permute-start | bytes 626696 | tf_op jit(solution)/shard_map/ppermute | solution.py:302
  47.4 8.2 %collective-permute-start.19 = (f32[136,384]{1,0:T(8,128)S(1)}, f32[136,384]{1,0:T(8,128)S(1)}, u32[]{:S(2)}, u32[]{:S(2)}) collective-permute-start(f32[136,384]{1,0:T(8,128)S(1)} %get-tuple-element.102.send), channel_id=1, source_target_pairs={{0,192},{1,193},{2,194},{3,195},{4,196},{5,197},{6,198},{7,199},{8... | collective-permute-start | bytes 626696 | tf_op jit(solution)/shard_map/ppermute | solution.py:302
  53.6 4.9 %collective-permute-start.12 = (f32[72,384]{1,0:T(8,128)S(1)}, f32[72,384]{1,0:T(8,128)S(1)}, u32[]{:S(2)}, u32[]{:S(2)}) collective-permute-start(f32[72,384]{1,0:T(8,128)S(1)} %get-tuple-element.88.send_1), channel_id=1, source_target_pairs={{0,6},{1,7},{2,4},{3,5},{4,2},{5,3},{6,0},{7,1},{8,14},{9,15},{10,... | collective-permute-start | bytes 331784 | tf_op jit(solution)/shard_map/ppermute | solution.py:302
  54.9 3.7 %collective-permute-start.14 = (f32[72,384]{1,0:T(8,128)S(1)}, f32[72,384]{1,0:T(8,128)S(1)}, u32[]{:S(2)}, u32[]{:S(2)}) collective-permute-start(f32[72,384]{1,0:T(8,128)S(1)} %get-tuple-element.92.send_2), channel_id=1, source_target_pairs={{0,2},{1,3},{2,0},{3,1},{4,6},{5,7},{6,4},{7,5},{8,10},{9,11},{10,... | collective-permute-start | bytes 331784 | tf_op jit(solution)/shard_map/ppermute | solution.py:302
  55.0 5.2 %collective-permute-start.18 = (f32[72,384]{1,0:T(8,128)S(1)}, f32[72,384]{1,0:T(8,128)S(1)}, u32[]{:S(2)}, u32[]{:S(2)}) collective-permute-start(f32[72,384]{1,0:T(8,128)S(1)} %get-tuple-element.100.send_1), channel_id=1, source_target_pairs={{0,192},{1,193},{2,194},{3,195},{4,196},{5,197},{6,198},{7,199},{8... | collective-permute-start | bytes 331784 | tf_op jit(solution)/shard_map/ppermute | solution.py:302
  55.6 4.6 %collective-permute-start.20 = (f32[72,384]{1,0:T(8,128)S(1)}, f32[72,384]{1,0:T(8,128)S(1)}, u32[]{:S(2)}, u32[]{:S(2)}) collective-permute-start(f32[72,384]{1,0:T(8,128)S(1)} %get-tuple-element.104.send_2), channel_id=1, source_target_pairs={{0,64},{1,65},{2,66},{3,67},{4,68},{5,69},{6,70},{7,71},{8,72},{9,... | collective-permute-start | bytes 331784 | tf_op jit(solution)/shard_map/ppermute | solution.py:302
  58.6 8.5 %collective-permute-start.15 = (f32[40,768]{1,0:T(8,128)S(1)}, f32[40,768]{1,0:T(8,128)S(1)}, u32[]{:S(2)}, u32[]{:S(2)}) collective-permute-start(f32[40,768]{1,0:T(8,128)S(1)} %get-tuple-element.94.send), channel_id=1, source_target_pairs={{0,64},{1,65},{2,66},{3,67},{4,68},{5,69},{6,70},{7,71},{8,72},{9,... | collective-permute-start | bytes 368648 | tf_op jit(solution)/shard_map/ppermute | solution.py:302
  60.3 8.5 %collective-permute-start.21 = (f32[40,768]{1,0:T(8,128)S(1)}, f32[40,768]{1,0:T(8,128)S(1)}, u32[]{:S(2)}, u32[]{:S(2)}) collective-permute-start(f32[40,768]{1,0:T(8,128)S(1)} %get-tuple-element.106.send), channel_id=1, source_target_pairs={{0,2},{1,3},{2,0},{3,1},{4,6},{5,7},{6,4},{7,5},{8,10},{9,11},{10,... | collective-permute-start | bytes 368648 | tf_op jit(solution)/shard_map/ppermute | solution.py:302
  63.5 28.7 %collective-permute-start.5 = (f32[192,512]{1,0:T(8,128)S(1)}, f32[192,512]{1,0:T(8,128)S(1)}, u32[]{:S(2)}, u32[]{:S(2)}) collective-permute-start(f32[192,512]{1,0:T(8,128)S(1)} %get-tuple-element.78), channel_id=1, source_target_pairs={{0,1},{1,0},{2,3},{3,2},{4,5},{5,4},{6,7},{7,6},{8,9},{9,8},{10,11... | collective-permute-start | bytes 1179656 | tf_op jit(solution)/shard_map/ppermute | solution.py:302
  67.1 5.1 %collective-permute-start.16 = (f32[24,768]{1,0:T(8,128)S(1)}, f32[24,768]{1,0:T(8,128)S(1)}, u32[]{:S(2)}, u32[]{:S(2)}) collective-permute-start(f32[24,768]{1,0:T(8,128)S(1)} %get-tuple-element.96.send_a), channel_id=1, source_target_pairs={{0,192},{1,193},{2,194},{3,195},{4,196},{5,197},{6,198},{7,199},{8... | collective-permute-start | bytes 221192 | tf_op jit(solution)/shard_map/ppermute | solution.py:302
  68.8 4.8 %collective-permute-start.22 = (f32[24,768]{1,0:T(8,128)S(1)}, f32[24,768]{1,0:T(8,128)S(1)}, u32[]{:S(2)}, u32[]{:S(2)}) collective-permute-start(f32[24,768]{1,0:T(8,128)S(1)} %get-tuple-element.108.send_b), channel_id=1, source_target_pairs={{0,6},{1,7},{2,4},{3,5},{4,2},{5,3},{6,0},{7,1},{8,14},{9,15},{10,... | collective-permute-start | bytes 221192 | tf_op jit(solution)/shard_map/ppermute | solution.py:302
  73.6 4.5 %collective-permute-start.24 = (f32[12,1536]{1,0:T(8,128)S(1)}, f32[12,1536]{1,0:T(8,128)S(1)}, u32[]{:S(2)}, u32[]{:S(2)}) collective-permute-start(f32[12,1536]{1,0:T(8,128)S(1)} %get-tuple-element.111), channel_id=1, source_target_pairs={{0,16},{1,17},{2,18},{3,19},{4,20},{5,21},{6,22},{7,23},{8,24},{9,... | collective-permute-start | bytes 221192 | tf_op jit(solution)/shard_map/ppermute | solution.py:302
  73.7 7.2 %collective-permute-start.25 = (f32[12,1536]{1,0:T(8,128)S(1)}, f32[12,1536]{1,0:T(8,128)S(1)}, u32[]{:S(2)}, u32[]{:S(2)}) collective-permute-start(f32[12,1536]{1,0:T(8,128)S(1)} %get-tuple-element.112), channel_id=1, source_target_pairs={{0,24},{1,25},{2,26},{3,27},{4,28},{5,29},{6,30},{7,31},{8,16},{9,... | collective-permute-start | bytes 221192 | tf_op jit(solution)/shard_map/ppermute | solution.py:302
  73.8 12.0 %collective-permute-start.23 = (f32[12,1536]{1,0:T(8,128)S(1)}, f32[12,1536]{1,0:T(8,128)S(1)}, u32[]{:S(2)}, u32[]{:S(2)}) collective-permute-start(f32[12,1536]{1,0:T(8,128)S(1)} %get-tuple-element.110.send), channel_id=1, source_target_pairs={{0,8},{1,9},{2,10},{3,11},{4,12},{5,13},{6,14},{7,15},{8,0},{9,1},... | collective-permute-start | bytes 221192 | tf_op jit(solution)/shard_map/ppermute | solution.py:302
  76.3 11.1 %collective-permute-start.9 = (f32[96,512]{1,0:T(8,128)S(1)}, f32[96,512]{1,0:T(8,128)S(1)}, u32[]{:S(2)}, u32[]{:S(2)}) collective-permute-start(f32[96,512]{1,0:T(8,128)S(1)} %get-tuple-element.82), channel_id=1, source_target_pairs={{0,255},{1,2},{2,1},{3,4},{4,3},{5,6},{6,5},{7,8},{8,7},{9,10},{10... | collective-permute-start | bytes 589832 | tf_op jit(solution)/shard_map/ppermute | solution.py:307
  78.2 13.0 %collective-permute-start.6 = (f32[96,512]{1,0:T(8,128)S(1)}, f32[96,512]{1,0:T(8,128)S(1)}, u32[]{:S(2)}, u32[]{:S(2)}) collective-permute-start(f32[96,512]{1,0:T(8,128)S(1)} %get-tuple-element.79), channel_id=1, source_target_pairs={{0,4},{1,5},{2,6},{3,7},{4,0},{5,1},{6,2},{7,3},{8,12},{9,13},{10,... | collective-permute-start | bytes 589832 | tf_op jit(solution)/shard_map/ppermute | solution.py:302
  80.9 10.3 %collective-permute-start.7 = (f32[96,512]{1,0:T(8,128)S(1)}, f32[96,512]{1,0:T(8,128)S(1)}, u32[]{:S(2)}, u32[]{:S(2)}) collective-permute-start(f32[96,512]{1,0:T(8,128)S(1)} %get-tuple-element.80), channel_id=1, source_target_pairs={{0,32},{1,33},{2,34},{3,35},{4,36},{5,37},{6,38},{7,39},{8,40},{9,... | collective-permute-start | bytes 589832 | tf_op jit(solution)/shard_map/ppermute | solution.py:302
  85.8 6.3 %collective-permute-start.8 = (f32[96,512]{1,0:T(8,128)S(1)}, f32[96,512]{1,0:T(8,128)S(1)}, u32[]{:S(2)}, u32[]{:S(2)}) collective-permute-start(f32[96,512]{1,0:T(8,128)S(1)} %get-tuple-element.81), channel_id=1, source_target_pairs={{0,128},{1,129},{2,130},{3,131},{4,132},{5,133},{6,134},{7,135},{8... | collective-permute-start | bytes 589832 | tf_op jit(solution)/shard_map/ppermute | solution.py:302
  87.5 13.9 %collective-permute-start.26 = (f32[10,1536]{1,0:T(8,128)S(1)}, f32[10,1536]{1,0:T(8,128)S(1)}, u32[]{:S(2)}, u32[]{:S(2)}) collective-permute-start(f32[10,1536]{1,0:T(8,128)S(1)} %get-tuple-element.114.send), channel_id=1, source_target_pairs={{0,48},{1,49},{2,50},{3,51},{4,52},{5,53},{6,54},{7,55},{8,56},{9,... | collective-permute-start | bytes 184328 | tf_op jit(solution)/shard_map/ppermute | solution.py:302
where the time goes:
time: 102 us
  starting transfers between devices  49.8 us (49%)
  waiting for transfers between devices  27.2 us (27%)
  Pallas kernels  21.6 us (21%)
  between operations  1.67 us (2%)
  local copies, waits for them, and re-layouts  1.65 us (2%)
    ppermute x25, starting transfers between devices, swap(): return lax.ppermute(value, 'edges', [(i, i ^ mask) for i in range(count)])  48.6 us
    ppermute x25, waiting for transfers between devices, swap(): return lax.ppermute(value, 'edges', [(i, i ^ mask) for i in range(count)])  27.1 us
    pallas_call x1, Pallas kernels, on_device_body(): call(middle, [((E, D), F32), ((E, D), F32), quarter, quarter, quarter, qu...  10.4 us
    pallas_call x1, Pallas kernels, on_device_body(): call(prepare, [((SLOTS, D), F32), ((SLOTS, D), F32), ((E, D), F32), ((WIN...  7.14 us
  transfers between devices with their start and end apart: 27, of which 11 were waited for; matrix products, arithmetic and copies ran while one was open for 0% of the time, Pallas kernels for 10%

commit v1 on v0

--- a/solution.py
+++ b/solution.py
@@ -35,9 +35,23 @@
     return op(a[0], b[0]) + (op(a[1], b[0]) + op(a[0], b[1]))
 
 
-def onehot(values, base, lanes):
-    shifted = (values - float(base)).astype(BF16)
-    return jnp.where(shifted == lanes, jnp.ones_like(lanes), jnp.zeros_like(lanes))
+def onehot(values, lanes):
+    return jnp.where(values == lanes, jnp.ones_like(lanes), jnp.zeros_like(lanes))
+
+
+def tall(row):
+    return jnp.broadcast_to(row.astype(F32), (128, 128))
+
+
+def onehots(row, blocks, lane, sub, put_rows, put_columns):
+    low, high = row & 127, row >> 7
+    base = onehot(tall(low).astype(BF16), sub)
+    for k in range(blocks):
+        put_rows(k, base * tall(high == k).astype(BF16))
+    base = onehot(jnp.transpose(tall(low)).astype(BF16), lane)
+    high = jnp.transpose(tall(high)).astype(BF16)
+    for k in range(blocks):
+        put_columns(k, jnp.where(high == jnp.full_like(high, k), base, jnp.zeros_like(base)))
 
 
 def prepare(
@@ -61,35 +75,40 @@
         u = jnp.where(w < HALO, low, jnp.where(w >= E + HALO, high, w - HALO))
         t = ints[:, pl.ds(pl.multiple_of(SLOTS + j * 128, 128), 128)] + blocks[j] * 128
         t = jnp.where(j < n_live, t, -1)
-        ub = jnp.broadcast_to(u.astype(F32), (128, 128))
-        tb = jnp.broadcast_to(t.astype(F32), (128, 128))
-        for k in range(5):
+
+        def put_ot(k, hit):
             rows = 128 if k < 4 else 64
-            ot[k * 128 : k * 128 + rows, at] = onehot(ub, k * 128, sub)[:rows]
-        for k in range(3):
-            tt[k * 128 : k * 128 + 128, at] = onehot(tb, k * 128, sub)
-        uc = jnp.transpose(ub)
-        tc = jnp.transpose(tb)
-        for k in range(5):
-            hit = onehot(uc, k * 128, lane)
+            ot[k * 128 : k * 128 + rows, at] = hit[:rows]
+
+        def put_ow(k, hit):
             ow[at, k * 128 : k * 128 + 128] = hit
             ow[at, PAD + k * 128 : PAD + k * 128 + 128] = hit
-        for k in range(3):
-            hit = onehot(tc, k * 128, lane)
+
+        def put_tt(k, hit):
+            tt[k * 128 : k * 128 + 128, at] = hit
+
+        def put_t2(k, hit):
             t2[at, k * 128 : k * 128 + 128] = hit
             t2[at, E + k * 128 : E + k * 128 + 128] = hit
+
+        onehots(u, 5, lane, sub, put_ot, put_ow)
+        onehots(t, 3, lane, sub, put_tt, put_t2)
         return carry
 
     lax.fori_loop(0, TILES, tile, 0)
     position = lax.broadcasted_iota(I32, (1, E), 1)
     group = (position >= HALO).astype(I32) + (position >= 2 * HALO).astype(I32) + (position >= 3 * HALO).astype(I32)
-    partner_row = (ints[:, 2 * SLOTS :] + group * HALO).astype(F32)
+    partner_row = ints[:, 2 * SLOTS :] + group * HALO
     for k in range(3):
-        pb = jnp.broadcast_to(partner_row[:, k * 128 : k * 128 + 128], (128, 128))
-        pc = jnp.transpose(pb)
-        for i in range(3):
-            rt[i * 128 : i * 128 + 128, k * 128 : k * 128 + 128] = onehot(pb, i * 128, sub)
-            r[k * 128 : k * 128 + 128, i * 128 : i * 128 + 128] = onehot(pc, i * 128, lane)
+        at = slice(k * 128, k * 128 + 128)
+
+        def put_rt(i, hit, at=at):
+            rt[i * 128 : i * 128 + 128, at] = hit
+
+        def put_r(i, hit, at=at):
+            r[at, i * 128 : i * 128 + 128] = hit
+
+        onehots(partner_row[:, at], 3, lane, sub, put_rt, put_r)
     row = lax.broadcasted_iota(I32, (1, D), 1)
     j = jnp.bitwise_xor(row >> 1, me[0])
     bit = [(j >> b) & 1 for b in range(8)]
@@ -249,35 +268,54 @@
     halves(keep[...] + got[:n], send[n:] + got[n:], keep_next, send_next)
 
 
-def fold_join(keep_a, send_a, got_a, keep_b, send_b, got_b, keep_next, send_1, send_2, send_3):
+BASIS = 2 * D
+
+
+def fold_join(keep_a, send_a, got_a, keep_b, send_b, got_b, keep_next, send_next):
     n = keep_a.shape[0]
-    for at, keep, send, got in ((slice(0, HALF), keep_a, send_a, got_a), (slice(HALF, 2 * HALF), keep_b, send_b, got_b)):
+    for at, keep, send, got in ((0, keep_a, send_a, got_a), (HALF, keep_b, send_b, got_b)):
         rows = keep[...] + got[:n]
         extra = send[n:] + got[n:]
-        keep_next[:, at] = rows[:4]
-        for k, ref in ((8, send_1), (4, send_2), (12, send_3)):
-            ref[:4, at] = rows[k : k + 4]
-            ref[4:, at] = extra
-
-
-def fold_four(keep, send, got_1, got_2, got_3, keep_next, send_next):
-    rows = (keep[...] + got_2[:4]) + (got_1[:4] + got_3[:4])
-    extra = (send[4:] + got_2[4:]) + (got_1[4:] + got_3[4:])
-    halves(rows, extra, keep_next, send_next)
+        width = min(HALF, BASIS - at)
+        keep_next[:, at : at + HALF] = rows[:8]
+        send_next[:, at : at + width] = extra[:, :width]
+        send_next[:, BASIS + at : BASIS + at + HALF] = rows[8:]
+
+
+def fold_z0(keep, send, got, keep_next, send_next):
+    rows = keep[...] + got[:, BASIS:]
+    keep_next[...] = rows[:4]
+    send_next[:, :BASIS] = send[:, :BASIS] + got[:, :BASIS]
+    send_next[:4, BASIS:] = rows[4:, :HALF]
+    send_next[4:, BASIS:] = rows[4:, HALF:]
+
+
+def fold_z1(keep, send, got, keep_next, send_next):
+    send_next[:, :BASIS] = send[:, :BASIS] + got[:, :BASIS]
+    for k in range(2):
+        rows = keep[:, k * HALF : k * HALF + HALF] + got[4 * k : 4 * k + 4, BASIS:]
+        keep_next[:, k * HALF : k * HALF + HALF] = rows[:2]
+        for i in range(2):
+            q = 2 * k + i
+            send_next[2 * q : 2 * q + 2, BASIS:] = rows[2:, i * PART : i * PART + PART]
 
 
 def fold_last(keep, send, got, layers, rev, basis):
-    rows = keep[...] + got[:2]
-    extra = send[2:] + got[2:]
-    for k in range(3):
-        for a in range(2):
-            piece = rows[a : a + 1, k * D : k * D + D]
-            if k < 2:
-                layers[k : k + 1, a * D : a * D + D] = piece
-            else:
-                rev[:, a * D : a * D + D] = piece
+    extra = send[:, :BASIS] + got[:, :BASIS]
     basis[:8] = extra[:, :D]
-    basis[8:] = extra[:, D : 2 * D]
+    basis[8:] = extra[:, D:]
+    for q in range(4):
+        rows = keep[:, q * PART : q * PART + PART] + got[2 * q : 2 * q + 2, BASIS:]
+        for k in range(3):
+            first, last = max(q * PART, k * D), min(q * PART + PART, k * D + D)
+            for a in range(2):
+                if first < last:
+                    piece = rows[a : a + 1, first - q * PART : last - q * PART]
+                    at = a * D + first - k * D
+                    if k < 2:
+                        layers[k : k + 1, at : at + last - first] = piece
+                    else:
+                        rev[:, at : at + last - first] = piece
 
 
 def call(kernel, outs, specs, scratch=(), flops=1_000_000, grant=8):
@@ -388,11 +426,9 @@
     got_a, got_b = swap(a[1], 64), swap(b[1], 2)
     a, b = step(a, got_a), step(b, got_b)
     got_a, got_b = swap(a[1], 192), swap(b[1], 6)
-    keep, send_1, send_2, send_3 = call(fold_join, [((4, 3 * D), F32)] + [((12, 3 * D), F32)] * 3, "v" * 6)(
-        *a, got_a, *b, got_b
-    )
-    got_1, got_2, got_3 = swap(send_1, 8), swap(send_2, 16), swap(send_3, 24)
-    c = call(fold_four, [((2, 3 * D), F32), ((10, 3 * D), F32)], "v" * 5)(keep, send_1, got_1, got_2, got_3)
+    c = call(fold_join, [((8, 3 * D), F32), ((8, BASIS + 3 * D), F32)], "v" * 6)(*a, got_a, *b, got_b)
+    c = call(fold_z0, [((4, 3 * D), F32), ((8, BASIS + HALF), F32)], "vvv")(*c, swap(c[1], 8))
+    c = call(fold_z1, [((2, 3 * D), F32), ((8, BASIS + PART), F32)], "vvv")(*c, swap(c[1], 16))
     got = tie(swap(c[1], 48), grad_messages)
     layers, rev, basis = call(fold_last, [((2, 2 * D), F32), ((1, 2 * D), F32), ((16, D), F32)], "vvv")(*c, got)
     return (out, grad_messages, layers, rev.reshape(2 * D), basis)

time: 102 us -> 103 us (level)
  the two profiles are of different devices: /device:TPU:1 before, /device:TPU:64 now
where the time goes in v1:
time: 103 us
  starting transfers between devices  57.3 us (56%)
  Pallas kernels  21.7 us (21%)
  waiting for transfers between devices  20.8 us (20%)
  local copies, waits for them, and re-layouts  1.65 us (2%)
  between operations  1.62 us (2%)
    ppermute x24, starting transfers between devices, swap(): return lax.ppermute(value, 'edges', [(i, i ^ mask) for i in range(count)])  54.9 us
    ppermute x24, waiting for transfers between devices, swap(): return lax.ppermute(value, 'edges', [(i, i ^ mask) for i in range(count)])  19.3 us
    pallas_call x1, Pallas kernels, on_device_body(): call(middle, [((E, D), F32), ((E, D), F32), quarter, quarter, quarter, qu...  10.4 us
    pallas_call x1, Pallas kernels, on_device_body(): call(prepare, [((SLOTS, D), F32), ((SLOTS, D), F32), ((E, D), F32), ((WIN...  7.27 us
    ppermute x2, starting transfers between devices, swap_side(): lax.ppermute(value, 'edges', [(i, (i + (1 if i % 2 else -1)) % count) for...  2.41 us
  transfers between devices with their start and end apart: 26, of which 13 were waited for; matrix products, arithmetic and copies ran while one was open for 0% of the time, Pallas kernels for 10%

profile of v1, /device:TPU:64, one launch (start us, length us, event | category | flops | bytes accessed | tf_op | source)
XLA Modules:
  0.0 103.1 jit_solution(16718561172024127558)
XLA Ops:
  0.7 1.6 %constant_dynamic-slice_fusion = (f32[96,512]{1,0:T(8,128)S(1)}, f32[96,512]{1,0:T(8,128)S(1)}, f32[96,512]{1,0:T(8,128)S(1)}, f32[96,512]{1,0:T(8,128)S(1)}, f32[96,512]{1,0:T(8,128)S(1)}, /*index=5*/f32[96,512]{1,0:T(8,128)S(1)}) fusion(f32[384,512]{1,0:T(8,128)} %m.3, s32[]{:T(128)S(6)} %select_n.7, s32[]{:T(128)S(6)} %select_n.6), kind=kLoop, calls=%fused_computation.2 | loop fusion | bytes 2359304 | tf_op jit(solution)/shard_map/dynamic_slice | solution.py:364
  2.4 0.1 collective-permute-start
  2.5 2.4 %collective-permute-start.4 = (f32[96,512]{1,0:T(8,128)S(1)}, f32[96,512]{1,0:T(8,128)S(1)}, u32[]{:S(2)}, u32[]{:S(2)}) collective-permute-start(f32[96,512]{1,0:T(8,128)S(1)} %get-tuple-element.119), channel_id=1, source_target_pairs={{0,255},{1,2},{2,1},{3,4},{4,3},{5,6},{6,5},{7,8},{8,7},{9,10},{10... | collective-permute-start | bytes 589832 | tf_op jit(solution)/shard_map/ppermute | solution.py:345
  4.9 3.2 %collective-permute-start.3 = (f32[96,512]{1,0:T(8,128)S(1)}, f32[96,512]{1,0:T(8,128)S(1)}, u32[]{:S(2)}, u32[]{:S(2)}) collective-permute-start(f32[96,512]{1,0:T(8,128)S(1)} %get-tuple-element.120), channel_id=1, source_target_pairs={{0,128},{1,129},{2,130},{3,131},{4,132},{5,133},{6,134},{7,135},{8... | collective-permute-start | bytes 589832 | tf_op jit(solution)/shard_map/ppermute | solution.py:340
  8.1 6.3 %collective-permute-start.2 = (f32[96,512]{1,0:T(8,128)S(1)}, f32[96,512]{1,0:T(8,128)S(1)}, u32[]{:S(2)}, u32[]{:S(2)}) collective-permute-start(f32[96,512]{1,0:T(8,128)S(1)} %get-tuple-element.121), channel_id=1, source_target_pairs={{0,32},{1,33},{2,34},{3,35},{4,36},{5,37},{6,38},{7,39},{8,40},{9,... | collective-permute-start | bytes 589832 | tf_op jit(solution)/shard_map/ppermute | solution.py:340
  14.3 0.4 collective-permute-start.1
  15.4 0.0 collective-permute-done.core_in
  15.5 0.0 copy-start.2
  15.5 0.0 copy-start.3
  15.5 7.3 %shard_map.146 = (f32[1536,512]{1,0:T(8,128)S(1)}, f32[1536,512]{1,0:T(8,128)S(1)}, f32[384,512]{1,0:T(8,128)S(1)}, bf16[576,1536]{1,0:T(8,128)(2,1)S(1)}, bf16[...) custom-call(s32[1]{0:T(128)} %bitcast.me, ...), custom_call_target="tpu_custom_call" | custom-call | flops 4000000000 | bytes 1048576 | tf_op jit(solution)/shard_map/pallas_call | solution.py:371
  22.8 10.4 %shard_map.147 = (f32[384,512]{1,0:T(8,128)}, f32[384,512]{1,0:T(8,128)S(1)}, f32[96,512]{1,0:T(8,128)S(1)}, f32[96,512]{1,0:T(8,128)S(1)}, f32[96,512]{1,0:T(8,...) custom-call(f32[192,512]{1,0:T(8,128)S(1)} %collective-permute-done., ...), custom_call_target="tpu_custom_call" | custom-call | flops 16000000000 | bytes 1048576 | tf_op jit(solution)/shard_map/pallas_call | solution.py:388
  33.2 0.0 collective-permute-start.10
  33.3 3.5 %collective-permute-done.10.got = f32[264,1536]{1,0:T(8,128)S(1)} collective-permute-done((f32[264,1536]{1,0:T(8,128)S(1)}, f32[264,1536]{1,0:T(8,128)S(1)}, u32[]{:S(2)}, u32[]{:S(2)}) %collective-permute-start.10) | collective-permute-done | bytes 1622048 | tf_op jit(solution)/shard_map/ppermute | solution.py:340
  36.7 0.2 shard_map.150
  36.9 1.0 collective-permute-start.11
  37.9 2.9 %collective-permute-start.13 = (f32[136,384]{1,0:T(8,128)S(1)}, f32[136,384]{1,0:T(8,128)S(1)}, u32[]{:S(2)}, u32[]{:S(2)}) collective-permute-start(f32[136,384]{1,0:T(8,128)S(1)} %get-tuple-element.90.send), channel_id=1, source_target_pairs={{0,6},{1,7},{2,4},{3,5},{4,2},{5,3},{6,0},{7,1},{8,14},{9,15},{10,... | collective-permute-start | bytes 626696 | tf_op jit(solution)/shard_map/ppermute | solution.py:340
  40.7 0.7 collective-permute-start.17
  41.4 0.4 collective-permute-start.19
  41.8 2.4 %collective-permute-done.11.got = f32[136,384]{1,0:T(8,128)S(1)} collective-permute-done((f32[136,384]{1,0:T(8,128)S(1)}, f32[136,384]{1,0:T(8,128)S(1)}, u32[]{:S(2)}, u32[]{:S(2)}) %collective-permute-start.11) | collective-permute-done | bytes 208928 | tf_op jit(solution)/shard_map/ppermute | solution.py:340
  44.2 2.2 %collective-permute-start.12 = (f32[72,384]{1,0:T(8,128)S(1)}, f32[72,384]{1,0:T(8,128)S(1)}, u32[]{:S(2)}, u32[]{:S(2)}) collective-permute-start(f32[72,384]{1,0:T(8,128)S(1)} %get-tuple-element.88.send_1), channel_id=1, source_target_pairs={{0,6},{1,7},{2,4},{3,5},{4,2},{5,3},{6,0},{7,1},{8,14},{9,15},{10,... | collective-permute-start | bytes 331784 | tf_op jit(solution)/shard_map/ppermute | solution.py:340
  46.4 1.1 %collective-permute-start.14 = (f32[72,384]{1,0:T(8,128)S(1)}, f32[72,384]{1,0:T(8,128)S(1)}, u32[]{:S(2)}, u32[]{:S(2)}) collective-permute-start(f32[72,384]{1,0:T(8,128)S(1)} %get-tuple-element.92.send_2), channel_id=1, source_target_pairs={{0,2},{1,3},{2,0},{3,1},{4,6},{5,7},{6,4},{7,5},{8,10},{9,11},{10,... | collective-permute-start | bytes 331784 | tf_op jit(solution)/shard_map/ppermute | solution.py:340
  47.6 1.1 %collective-permute-start.18 = (f32[72,384]{1,0:T(8,128)S(1)}, f32[72,384]{1,0:T(8,128)S(1)}, u32[]{:S(2)}, u32[]{:S(2)}) collective-permute-start(f32[72,384]{1,0:T(8,128)S(1)} %get-tuple-element.100.send_1), channel_id=1, source_target_pairs={{0,192},{1,193},{2,194},{3,195},{4,196},{5,197},{6,198},{7,199},{8... | collective-permute-start | bytes 331784 | tf_op jit(solution)/shard_map/ppermute | solution.py:340
  48.7 0.2 collective-permute-done.19.got
  49.0 0.2 collective-permute-start.20
  49.2 1.0 %collective-permute-done.12.got_1 = f32[72,384]{1,0:T(8,128)S(1)} collective-permute-done((f32[72,384]{1,0:T(8,128)S(1)}, f32[72,384]{1,0:T(8,128)S(1)}, u32[]{:S(2)}, u32[]{:S(2)}) %collective-permute-start.12) | collective-permute-done | bytes 110624 | tf_op jit(solution)/shard_map/ppermute | solution.py:340
  50.3 1.0 collective-permute-done.14.got_2
  51.3 0.8 collective-permute-start.15
  52.1 1.5 %collective-permute-done.18.got_1 = f32[72,384]{1,0:T(8,128)S(1)} collective-permute-done((f32[72,384]{1,0:T(8,128)S(1)}, f32[72,384]{1,0:T(8,128)S(1)}, u32[]{:S(2)}, u32[]{:S(2)}) %collective-permute-start.18) | collective-permute-done | bytes 110624 | tf_op jit(solution)/shard_map/ppermute | solution.py:340
  53.6 1.0 collective-permute-done.20.got_2
  54.7 1.0 collective-permute-start.21
  55.6 0.7 collective-permute-done.15.got
  56.3 1.3 %collective-permute-start.16 = (f32[24,768]{1,0:T(8,128)S(1)}, f32[24,768]{1,0:T(8,128)S(1)}, u32[]{:S(2)}, u32[]{:S(2)}) collective-permute-start(f32[24,768]{1,0:T(8,128)S(1)} %get-tuple-element.96.send_a), channel_id=1, source_target_pairs={{0,192},{1,193},{2,194},{3,195},{4,196},{5,197},{6,198},{7,199},{8... | collective-permute-start | bytes 221192 | tf_op jit(solution)/shard_map/ppermute | solution.py:340
  57.6 2.0 %collective-permute-done.21.got = f32[40,768]{1,0:T(8,128)S(1)} collective-permute-done((f32[40,768]{1,0:T(8,128)S(1)}, f32[40,768]{1,0:T(8,128)S(1)}, u32[]{:S(2)}, u32[]{:S(2)}) %collective-permute-start.21) | collective-permute-done | bytes 122912 | tf_op jit(solution)/shard_map/ppermute | solution.py:340
  59.6 1.0 collective-permute-start.22
  60.6 2.0 %shard_map.148 = (f32[384,512]{1,0:T(8,128)S(1)}, f32[192,512]{1,0:T(8,128)S(1)}, f32[96,512]{1,0:T(8,128)S(1)}) custom-call(bf16[576,1536]{1,0:T(8,128)(2,1)S(1)} %get-tuple-element.72.ot, bf16[1536,512]{1,0:T(8,128)(2,1)S(1)} %get-tuple-element.73.wt_hi, bf16[1536,512]{1,0:T(8,128)(2,1)S(1)} %get-tuple-element.74.wt_lo, ...), custom_call_target="tpu_custom_call" | custom-call | flops 1000000000 | bytes 1048576 | tf_op jit(solution)/shard_map/pallas_call | solution.py:407
  62.6 0.1 collective-permute-start.5
  62.7 2.6 %collective-permute-done.22.got_b = f32[24,768]{1,0:T(8,128)S(1)} collective-permute-done((f32[24,768]{1,0:T(8,128)S(1)}, f32[24,768]{1,0:T(8,128)S(1)}, u32[]{:S(2)}, u32[]{:S(2)}) %collective-permute-start.22) | collective-permute-done | bytes 73760 | tf_op jit(solution)/shard_map/ppermute | solution.py:340
  65.3 3.7 %collective-permute-start.23 = (f32[8,2560]{1,0:T(8,128)S(1)}, f32[8,2560]{1,0:T(8,128)S(1)}, u32[]{:S(2)}, u32[]{:S(2)}) collective-permute-start(f32[8,2560]{1,0:T(8,128)S(1)} %get-tuple-element.110.send), channel_id=1, source_target_pairs={{0,8},{1,9},{2,10},{3,11},{4,12},{5,13},{6,14},{7,15},{8,0},{9,1},... | collective-permute-start | bytes 245768 | tf_op jit(solution)/shard_map/ppermute | solution.py:340
  69.0 2.4 %collective-permute-done.23.got = f32[8,2560]{1,0:T(8,128)S(1)} collective-permute-done((f32[8,2560]{1,0:T(8,128)S(1)}, f32[8,2560]{1,0:T(8,128)S(1)}, u32[]{:S(2)}, u32[]{:S(2)}) %collective-permute-start.23) | collective-permute-done | bytes 81952 | tf_op jit(solution)/shard_map/ppermute | solution.py:340
  71.4 5.2 %collective-permute-start.24 = (f32[8,1792]{1,0:T(8,128)S(1)}, f32[8,1792]{1,0:T(8,128)S(1)}, u32[]{:S(2)}, u32[]{:S(2)}) collective-permute-start(f32[8,1792]{1,0:T(8,128)S(1)} %get-tuple-element.112.send), channel_id=1, source_target_pairs={{0,16},{1,17},{2,18},{3,19},{4,20},{5,21},{6,22},{7,23},{8,24},{9,... | collective-permute-start | bytes 172040 | tf_op jit(solution)/shard_map/ppermute | solution.py:340
  76.6 1.6 %collective-permute-start.6 = (f32[96,512]{1,0:T(8,128)S(1)}, f32[96,512]{1,0:T(8,128)S(1)}, u32[]{:S(2)}, u32[]{:S(2)}) collective-permute-start(f32[96,512]{1,0:T(8,128)S(1)} %get-tuple-element.79), channel_id=1, source_target_pairs={{0,4},{1,5},{2,6},{3,7},{4,0},{5,1},{6,2},{7,3},{8,12},{9,13},{10,... | collective-permute-start | bytes 589832 | tf_op jit(solution)/shard_map/ppermute | solution.py:340
  78.2 5.2 %collective-permute-start.7 = (f32[96,512]{1,0:T(8,128)S(1)}, f32[96,512]{1,0:T(8,128)S(1)}, u32[]{:S(2)}, u32[]{:S(2)}) collective-permute-start(f32[96,512]{1,0:T(8,128)S(1)} %get-tuple-element.80), channel_id=1, source_target_pairs={{0,32},{1,33},{2,34},{3,35},{4,36},{5,37},{6,38},{7,39},{8,40},{9,... | collective-permute-start | bytes 589832 | tf_op jit(solution)/shard_map/ppermute | solution.py:340
  83.3 0.6 collective-permute-start.8
  83.9 1.4 %collective-permute-done.9.side_in = f32[96,512]{1,0:T(8,128)S(1)} collective-permute-done((f32[96,512]{1,0:T(8,128)S(1)}, f32[96,512]{1,0:T(8,128)S(1)}, u32[]{:S(2)}, u32[]{:S(2)}) %collective-permute-start.9) | collective-permute-done | bytes 196640 | tf_op jit(solution)/shard_map/ppermute | solution.py:345
  85.4 15.1 %collective-permute-start.25 = (f32[8,1408]{1,0:T(8,128)S(1)}, f32[8,1408]{1,0:T(8,128)S(1)}, u32[]{:S(2)}, u32[]{:S(2)}) collective-permute-start(f32[8,1408]{1,0:T(8,128)S(1)} %get-tuple-element.114.send), channel_id=1, source_target_pairs={{0,48},{1,49},{2,50},{3,51},{4,52},{5,53},{6,54},{7,55},{8,56},{9,... | collective-permute-start | bytes 135176 | tf_op jit(solution)/shard_map/ppermute | solution.py:340
  100.5 1.0 shard_map.149
  101.5 1.0 collective-permute-done.25.got
  102.5 0.6 shard_map.162
  (45 shorter events, 0.4 us)
Async XLA Ops:
  0.6 14.8 %copy-start = (f32[384,512]{1,0:T(8,128)S(1)}, f32[384,512]{1,0:T(8,128)}, u32[]{:S(2)}) copy-start(f32[384,512]{1,0:T(8,128)} %m.3) | copy-start | bytes 2359300
  0.6 14.7 %copy-start.7 = (s32[1536]{0:T(1024)S(1)}, s32[1536]{0:T(1024)}, u32[]{:S(2)}) copy-start(s32[1536]{0:T(1024)} %param.15) | copy-start | bytes 18436
  0.7 14.7 %copy-start.8 = (s32[1536]{0:T(1024)S(1)}, s32[1536]{0:T(1024)}, u32[]{:S(2)}) copy-start(s32[1536]{0:T(1024)} %param.14) | copy-start | bytes 18436
  0.7 14.7 %copy-start.9 = (s32[384]{0:T(512)S(1)}, s32[384]{0:T(512)}, u32[]{:S(2)}) copy-start(s32[384]{0:T(512)} %param.12) | copy-start | bytes 4612
  0.7 14.8 %copy-start.4 = (f32[16,1536]{1,0:T(8,128)S(1)}, f32[16,1536]{1,0:T(8,128)}, u32[]{:S(2)}) copy-start(f32[16,1536]{1,0:T(8,128)} %coeffs.3) | copy-start | bytes 294916
  0.7 14.8 %copy-start.1 = (f32[2,512,512]{2,1,0:T(8,128)S(1)}, f32[2,512,512]{2,1,0:T(8,128)}, u32[]{:S(2)}) copy-start(f32[2,512,512]{2,1,0:T(8,128)} %wl.1) | copy-start | bytes 6291460
  0.7 14.8 %copy-start.5 = (f32[16,512]{1,0:T(8,128)S(1)}, f32[16,512]{1,0:T(8,128)}, u32[]{:S(2)}) copy-start(f32[16,512]{1,0:T(8,128)} %wb.1) | copy-start | bytes 98308
  0.7 14.8 %copy-start.6 = (s32[12]{0:T(128)S(1)}, s32[12]{0:T(128)}, u32[]{:S(2)}) copy-start(s32[12]{0:T(128)} %blocks.1) | copy-start | bytes 148
  2.4 13.1 %collective-permute-start = (f32[192,512]{1,0:T(8,128)S(1)}, f32[192,512]{1,0:T(8,128)S(1)}, u32[]{:S(2)}, u32[]{:S(2)}) collective-permute-start(f32[192,512]{1,0:T(8,128)S(1)} %pad_maximum_fusion), channel_id=1, source_target_pairs={{0,1},{1,0},{2,3},{3,2},{4,5},{5,4},{6,7},{7,6},{8,9},{9,8},{10,11... | collective-permute-start | bytes 1179656 | tf_op jit(solution)/shard_map/ppermute | solution.py:340
  2.5 13.0 %collective-permute-start.4 = (f32[96,512]{1,0:T(8,128)S(1)}, f32[96,512]{1,0:T(8,128)S(1)}, u32[]{:S(2)}, u32[]{:S(2)}) collective-permute-start(f32[96,512]{1,0:T(8,128)S(1)} %get-tuple-element.119), channel_id=1, source_target_pairs={{0,255},{1,2},{2,1},{3,4},{4,3},{5,6},{6,5},{7,8},{8,7},{9,10},{10... | collective-permute-start | bytes 589832 | tf_op jit(solution)/shard_map/ppermute | solution.py:345
  4.9 17.9 %collective-permute-start.3 = (f32[96,512]{1,0:T(8,128)S(1)}, f32[96,512]{1,0:T(8,128)S(1)}, u32[]{:S(2)}, u32[]{:S(2)}) collective-permute-start(f32[96,512]{1,0:T(8,128)S(1)} %get-tuple-element.120), channel_id=1, source_target_pairs={{0,128},{1,129},{2,130},{3,131},{4,132},{5,133},{6,134},{7,135},{8... | collective-permute-start | bytes 589832 | tf_op jit(solution)/shard_map/ppermute | solution.py:340
  8.1 14.8 %collective-permute-start.2 = (f32[96,512]{1,0:T(8,128)S(1)}, f32[96,512]{1,0:T(8,128)S(1)}, u32[]{:S(2)}, u32[]{:S(2)}) collective-permute-start(f32[96,512]{1,0:T(8,128)S(1)} %get-tuple-element.121), channel_id=1, source_target_pairs={{0,32},{1,33},{2,34},{3,35},{4,36},{5,37},{6,38},{7,39},{8,40},{9,... | collective-permute-start | bytes 589832 | tf_op jit(solution)/shard_map/ppermute | solution.py:340
  14.3 8.5 %collective-permute-start.1 = (f32[96,512]{1,0:T(8,128)S(1)}, f32[96,512]{1,0:T(8,128)S(1)}, u32[]{:S(2)}, u32[]{:S(2)}) collective-permute-start(f32[96,512]{1,0:T(8,128)S(1)} %get-tuple-element.122), channel_id=1, source_target_pairs={{0,4},{1,5},{2,6},{3,7},{4,0},{5,1},{6,2},{7,3},{8,12},{9,13},{10,... | collective-permute-start | bytes 589832 | tf_op jit(solution)/shard_map/ppermute | solution.py:340
  15.5 7.3 %copy-start.2 = (f32[512,512]{1,0:T(8,128)S(1)}, f32[512,512]{1,0:T(8,128)}, u32[]{:S(2)}) copy-start(f32[512,512]{1,0:T(8,128)} %wr.1) | copy-start | bytes 3145732
  15.5 7.3 %copy-start.3 = (f32[384,512]{1,0:T(8,128)S(1)}, f32[384,512]{1,0:T(8,128)}, u32[]{:S(2)}) copy-start(f32[384,512]{1,0:T(8,128)} %cot.1) | copy-start | bytes 2359300
  33.2 3.5 %collective-permute-start.10 = (f32[264,1536]{1,0:T(8,128)S(1)}, f32[264,1536]{1,0:T(8,128)S(1)}, u32[]{:S(2)}, u32[]{:S(2)}) collective-permute-start(f32[264,1536]{1,0:T(8,128)S(1)} %get-tuple-element.84), channel_id=1, source_target_pairs={{0,1},{1,0},{2,3},{3,2},{4,5},{5,4},{6,7},{7,6},{8,9},{9,8},{10,11... | collective-permute-start | bytes 4866056 | tf_op jit(solution)/shard_map/ppermute | solution.py:340
  36.9 7.3 %collective-permute-start.11 = (f32[136,384]{1,0:T(8,128)S(1)}, f32[136,384]{1,0:T(8,128)S(1)}, u32[]{:S(2)}, u32[]{:S(2)}) collective-permute-start(f32[136,384]{1,0:T(8,128)S(1)} %get-tuple-element.86.send), channel_id=1, source_target_pairs={{0,2},{1,3},{2,0},{3,1},{4,6},{5,7},{6,4},{7,5},{8,10},{9,11},{10,... | collective-permute-start | bytes 626696 | tf_op jit(solution)/shard_map/ppermute | solution.py:340
  37.9 8.5 %collective-permute-start.13 = (f32[136,384]{1,0:T(8,128)S(1)}, f32[136,384]{1,0:T(8,128)S(1)}, u32[]{:S(2)}, u32[]{:S(2)}) collective-permute-start(f32[136,384]{1,0:T(8,128)S(1)} %get-tuple-element.90.send), channel_id=1, source_target_pairs={{0,6},{1,7},{2,4},{3,5},{4,2},{5,3},{6,0},{7,1},{8,14},{9,15},{10,... | collective-permute-start | bytes 626696 | tf_op jit(solution)/shard_map/ppermute | solution.py:340
  40.7 6.8 %collective-permute-start.17 = (f32[136,384]{1,0:T(8,128)S(1)}, f32[136,384]{1,0:T(8,128)S(1)}, u32[]{:S(2)}, u32[]{:S(2)}) collective-permute-start(f32[136,384]{1,0:T(8,128)S(1)} %get-tuple-element.98.send), channel_id=1, source_target_pairs={{0,64},{1,65},{2,66},{3,67},{4,68},{5,69},{6,70},{7,71},{8,72},{9,... | collective-permute-start | bytes 626696 | tf_op jit(solution)/shard_map/ppermute | solution.py:340
  41.4 7.6 %collective-permute-start.19 = (f32[136,384]{1,0:T(8,128)S(1)}, f32[136,384]{1,0:T(8,128)S(1)}, u32[]{:S(2)}, u32[]{:S(2)}) collective-permute-start(f32[136,384]{1,0:T(8,128)S(1)} %get-tuple-element.102.send), channel_id=1, source_target_pairs={{0,192},{1,193},{2,194},{3,195},{4,196},{5,197},{6,198},{7,199},{8... | collective-permute-start | bytes 626696 | tf_op jit(solution)/shard_map/ppermute | solution.py:340
  44.2 6.0 %collective-permute-start.12 = (f32[72,384]{1,0:T(8,128)S(1)}, f32[72,384]{1,0:T(8,128)S(1)}, u32[]{:S(2)}, u32[]{:S(2)}) collective-permute-start(f32[72,384]{1,0:T(8,128)S(1)} %get-tuple-element.88.send_1), channel_id=1, source_target_pairs={{0,6},{1,7},{2,4},{3,5},{4,2},{5,3},{6,0},{7,1},{8,14},{9,15},{10,... | collective-permute-start | bytes 331784 | tf_op jit(solution)/shard_map/ppermute | solution.py:340
  46.4 4.8 %collective-permute-start.14 = (f32[72,384]{1,0:T(8,128)S(1)}, f32[72,384]{1,0:T(8,128)S(1)}, u32[]{:S(2)}, u32[]{:S(2)}) collective-permute-start(f32[72,384]{1,0:T(8,128)S(1)} %get-tuple-element.92.send_2), channel_id=1, source_target_pairs={{0,2},{1,3},{2,0},{3,1},{4,6},{5,7},{6,4},{7,5},{8,10},{9,11},{10,... | collective-permute-start | bytes 331784 | tf_op jit(solution)/shard_map/ppermute | solution.py:340
  47.6 6.0 %collective-permute-start.18 = (f32[72,384]{1,0:T(8,128)S(1)}, f32[72,384]{1,0:T(8,128)S(1)}, u32[]{:S(2)}, u32[]{:S(2)}) collective-permute-start(f32[72,384]{1,0:T(8,128)S(1)} %get-tuple-element.100.send_1), channel_id=1, source_target_pairs={{0,192},{1,193},{2,194},{3,195},{4,196},{5,197},{6,198},{7,199},{8... | collective-permute-start | bytes 331784 | tf_op jit(solution)/shard_map/ppermute | solution.py:340
  49.0 5.6 %collective-permute-start.20 = (f32[72,384]{1,0:T(8,128)S(1)}, f32[72,384]{1,0:T(8,128)S(1)}, u32[]{:S(2)}, u32[]{:S(2)}) collective-permute-start(f32[72,384]{1,0:T(8,128)S(1)} %get-tuple-element.104.send_2), channel_id=1, source_target_pairs={{0,64},{1,65},{2,66},{3,67},{4,68},{5,69},{6,70},{7,71},{8,72},{9,... | collective-permute-start | bytes 331784 | tf_op jit(solution)/shard_map/ppermute | solution.py:340
  51.3 5.0 %collective-permute-start.15 = (f32[40,768]{1,0:T(8,128)S(1)}, f32[40,768]{1,0:T(8,128)S(1)}, u32[]{:S(2)}, u32[]{:S(2)}) collective-permute-start(f32[40,768]{1,0:T(8,128)S(1)} %get-tuple-element.94.send), channel_id=1, source_target_pairs={{0,64},{1,65},{2,66},{3,67},{4,68},{5,69},{6,70},{7,71},{8,72},{9,... | collective-permute-start | bytes 368648 | tf_op jit(solution)/shard_map/ppermute | solution.py:340
  54.7 5.0 %collective-permute-start.21 = (f32[40,768]{1,0:T(8,128)S(1)}, f32[40,768]{1,0:T(8,128)S(1)}, u32[]{:S(2)}, u32[]{:S(2)}) collective-permute-start(f32[40,768]{1,0:T(8,128)S(1)} %get-tuple-element.106.send), channel_id=1, source_target_pairs={{0,2},{1,3},{2,0},{3,1},{4,6},{5,7},{6,4},{7,5},{8,10},{9,11},{10,... | collective-permute-start | bytes 368648 | tf_op jit(solution)/shard_map/ppermute | solution.py:340
  56.3 6.4 %collective-permute-start.16 = (f32[24,768]{1,0:T(8,128)S(1)}, f32[24,768]{1,0:T(8,128)S(1)}, u32[]{:S(2)}, u32[]{:S(2)}) collective-permute-start(f32[24,768]{1,0:T(8,128)S(1)} %get-tuple-element.96.send_a), channel_id=1, source_target_pairs={{0,192},{1,193},{2,194},{3,195},{4,196},{5,197},{6,198},{7,199},{8... | collective-permute-start | bytes 221192 | tf_op jit(solution)/shard_map/ppermute | solution.py:340
  59.6 5.7 %collective-permute-start.22 = (f32[24,768]{1,0:T(8,128)S(1)}, f32[24,768]{1,0:T(8,128)S(1)}, u32[]{:S(2)}, u32[]{:S(2)}) collective-permute-start(f32[24,768]{1,0:T(8,128)S(1)} %get-tuple-element.108.send_b), channel_id=1, source_target_pairs={{0,6},{1,7},{2,4},{3,5},{4,2},{5,3},{6,0},{7,1},{8,14},{9,15},{10,... | collective-permute-start | bytes 221192 | tf_op jit(solution)/shard_map/ppermute | solution.py:340
  62.6 37.9 %collective-permute-start.5 = (f32[192,512]{1,0:T(8,128)S(1)}, f32[192,512]{1,0:T(8,128)S(1)}, u32[]{:S(2)}, u32[]{:S(2)}) collective-permute-start(f32[192,512]{1,0:T(8,128)S(1)} %get-tuple-element.78), channel_id=1, source_target_pairs={{0,1},{1,0},{2,3},{3,2},{4,5},{5,4},{6,7},{7,6},{8,9},{9,8},{10,11... | collective-permute-start | bytes 1179656 | tf_op jit(solution)/shard_map/ppermute | solution.py:340
  65.3 6.1 %collective-permute-start.23 = (f32[8,2560]{1,0:T(8,128)S(1)}, f32[8,2560]{1,0:T(8,128)S(1)}, u32[]{:S(2)}, u32[]{:S(2)}) collective-permute-start(f32[8,2560]{1,0:T(8,128)S(1)} %get-tuple-element.110.send), channel_id=1, source_target_pairs={{0,8},{1,9},{2,10},{3,11},{4,12},{5,13},{6,14},{7,15},{8,0},{9,1},... | collective-permute-start | bytes 245768 | tf_op jit(solution)/shard_map/ppermute | solution.py:340
  71.4 11.9 %collective-permute-start.24 = (f32[8,1792]{1,0:T(8,128)S(1)}, f32[8,1792]{1,0:T(8,128)S(1)}, u32[]{:S(2)}, u32[]{:S(2)}) collective-permute-start(f32[8,1792]{1,0:T(8,128)S(1)} %get-tuple-element.112.send), channel_id=1, source_target_pairs={{0,16},{1,17},{2,18},{3,19},{4,20},{5,21},{6,22},{7,23},{8,24},{9,... | collective-permute-start | bytes 172040 | tf_op jit(solution)/shard_map/ppermute | solution.py:340
  76.6 8.8 %collective-permute-start.9 = (f32[96,512]{1,0:T(8,128)S(1)}, f32[96,512]{1,0:T(8,128)S(1)}, u32[]{:S(2)}, u32[]{:S(2)}) collective-permute-start(f32[96,512]{1,0:T(8,128)S(1)} %get-tuple-element.82), channel_id=1, source_target_pairs={{0,255},{1,2},{2,1},{3,4},{4,3},{5,6},{6,5},{7,8},{8,7},{9,10},{10... | collective-permute-start | bytes 589832 | tf_op jit(solution)/shard_map/ppermute | solution.py:345
  76.6 23.9 %collective-permute-start.6 = (f32[96,512]{1,0:T(8,128)S(1)}, f32[96,512]{1,0:T(8,128)S(1)}, u32[]{:S(2)}, u32[]{:S(2)}) collective-permute-start(f32[96,512]{1,0:T(8,128)S(1)} %get-tuple-element.79), channel_id=1, source_target_pairs={{0,4},{1,5},{2,6},{3,7},{4,0},{5,1},{6,2},{7,3},{8,12},{9,13},{10,... | collective-permute-start | bytes 589832 | tf_op jit(solution)/shard_map/ppermute | solution.py:340
  78.2 22.3 %collective-permute-start.7 = (f32[96,512]{1,0:T(8,128)S(1)}, f32[96,512]{1,0:T(8,128)S(1)}, u32[]{:S(2)}, u32[]{:S(2)}) collective-permute-start(f32[96,512]{1,0:T(8,128)S(1)} %get-tuple-element.80), channel_id=1, source_target_pairs={{0,32},{1,33},{2,34},{3,35},{4,36},{5,37},{6,38},{7,39},{8,40},{9,... | collective-permute-start | bytes 589832 | tf_op jit(solution)/shard_map/ppermute | solution.py:340
  83.3 17.1 %collective-permute-start.8 = (f32[96,512]{1,0:T(8,128)S(1)}, f32[96,512]{1,0:T(8,128)S(1)}, u32[]{:S(2)}, u32[]{:S(2)}) collective-permute-start(f32[96,512]{1,0:T(8,128)S(1)} %get-tuple-element.81), channel_id=1, source_target_pairs={{0,128},{1,129},{2,130},{3,131},{4,132},{5,133},{6,134},{7,135},{8... | collective-permute-start | bytes 589832 | tf_op jit(solution)/shard_map/ppermute | solution.py:340
  85.4 17.1 %collective-permute-start.25 = (f32[8,1408]{1,0:T(8,128)S(1)}, f32[8,1408]{1,0:T(8,128)S(1)}, u32[]{:S(2)}, u32[]{:S(2)}) collective-permute-start(f32[8,1408]{1,0:T(8,128)S(1)} %get-tuple-element.114.send), channel_id=1, source_target_pairs={{0,48},{1,49},{2,50},{3,51},{4,52},{5,53},{6,54},{7,55},{8,56},{9,... | collective-permute-start | bytes 135176 | tf_op jit(solution)/shard_map/ppermute | solution.py:340

commit v2 on v1

--- a/solution.py
+++ b/solution.py
@@ -55,12 +55,15 @@
 
 
 def prepare(
-    me, count, blocks, ints, coeffs, wb, m, core_in, side_in, wl,
+    me, count, blocks, source, target, rev, coeffs, wb, m, core_in, side_in, wl,
     gath, tw, agg, ot, t2, r, rt, pick, wl_hi, wl_lo,
-    ow, w2, tt, th, tl, c3, w3, wl_s, sem,
+    ints, ow, w2, tt, th, tl, c3, w3, wl_s, sem,
 ):
     copy = pltpu.make_async_copy(wl, wl_s, sem)
     copy.start()
+    ints[:, :SLOTS] = source[...].reshape(1, SLOTS)
+    ints[:, SLOTS : 2 * SLOTS] = target[...].reshape(1, SLOTS)
+    ints[:, 2 * SLOTS :] = rev[...].reshape(1, E)
     lane = lax.broadcasted_iota(I32, (128, 128), 1).astype(F32).astype(BF16)
     sub = lax.broadcasted_iota(I32, (128, 128), 0).astype(F32).astype(BF16)
     n_live = count[0]
@@ -120,8 +123,8 @@
         place = 2 * place + b
     hits = jnp.broadcast_to(place, (D, D)) == lax.broadcasted_iota(I32, (D, D), 0)
     pick[...] = jnp.where(hits, 1.0, 0.0).astype(BF16)
-    for at, rows, source in ((0, E, m[...]), (E, HALO, core_in[HALO:, :]), (E + HALO, HALO, side_in[...])):
-        w2[at : at + rows], w2[PAD + at : PAD + at + rows] = split(source)
+    for at, rows, piece in ((0, E, m[...]), (E, HALO, core_in[HALO:, :]), (E + HALO, HALO, side_in[...])):
+        w2[at : at + rows], w2[PAD + at : PAD + at + rows] = split(piece)
     w2[WIN:PAD] = jnp.zeros((PAD - WIN, D), BF16)
     w2[PAD + WIN :] = jnp.zeros((PAD - WIN, D), BF16)
     high, low = split(coeffs[...])
@@ -367,7 +370,6 @@
     core_in = swap(jnp.concatenate([messages[:HALO], toward_core], axis=0), 1)
     a3 = swap(messages[3 * HALO :], 128)
     a1 = swap(messages[HALO : 2 * HALO], 4)
-    ints = jnp.concatenate([tri_source, tri_target, rev_slot]).reshape(1, 2 * SLOTS + E)
     (gath, tw, agg, ot, t2, r, rt, pick, wl_hi, wl_lo) = call(
         prepare,
         [
@@ -375,8 +377,9 @@
             ((E, E), BF16), ((E, E), BF16), ((D, D), BF16),
             ((2, D, D), BF16), ((2, D, D), BF16),
         ],
-        "sss" + "v" * 6 + "h",
+        "sss" + "v" * 8 + "h",
         [
+            pltpu.VMEM((1, 2 * SLOTS + E), I32),
             pltpu.VMEM((SLOTS, 2 * PAD), BF16), pltpu.VMEM((2 * PAD, D), BF16), pltpu.VMEM((E, SLOTS), BF16),
             pltpu.VMEM((SLOTS, D), BF16), pltpu.VMEM((SLOTS, D), BF16),
             pltpu.VMEM((48, SLOTS), BF16), pltpu.VMEM((48, D), BF16),
@@ -384,7 +387,7 @@
         ],
         flops=4_000_000_000,
         grant=26,
-    )(me, tile_count, tile_block, ints, tri_basis, w_basis, messages, core_in, side_in, w_layers)
+    )(me, tile_count, tile_block, tri_source, tri_target, rev_slot, tri_basis, w_basis, messages, core_in, side_in, w_layers)
     out, gmp, gr0, gr1, gr2, gr3, wt_hi, wt_lo, own, send = call(
         middle,
         [

time: 103 us -> 103 us (level)
  no operation moved by 1% of the time
where the time goes in v2:
time: 103 us
  starting transfers between devices  56.8 us (55%)
  Pallas kernels  21.5 us (21%)
  waiting for transfers between devices  21.3 us (21%)
  local copies, waits for them, and re-layouts  1.64 us (2%)
  between operations  1.6 us (2%)
    ppermute x24, starting transfers between devices, swap(): return lax.ppermute(value, 'edges', [(i, i ^ mask) for i in range(count)])  54.4 us
    ppermute x24, waiting for transfers between devices, swap(): return lax.ppermute(value, 'edges', [(i, i ^ mask) for i in range(count)])  19.9 us
    pallas_call x1, Pallas kernels, on_device_body(): call(middle, [((E, D), F32), ((E, D), F32), quarter, quarter, quarter, qu...  10.4 us
    pallas_call x1, Pallas kernels, on_device_body(): call(prepare, [((SLOTS, D), F32), ((SLOTS, D), F32), ((E, D), F32), ((WIN...  7.09 us
    ppermute x2, starting transfers between devices, swap_side(): lax.ppermute(value, 'edges', [(i, (i + (1 if i % 2 else -1)) % count) for...  2.41 us
  transfers between devices with their start and end apart: 26, of which 13 were waited for; matrix products, arithmetic and copies ran while one was open for 0% of the time, Pallas kernels for 10%

profile of v2, /device:TPU:64, one launch (start us, length us, event | category | flops | bytes accessed | tf_op | source)
XLA Modules:
  0.0 103.0 jit_solution(8017472750000159840)
XLA Ops:
  0.7 1.6 %constant_dynamic-slice_fusion = (f32[96,512]{1,0:T(8,128)S(1)}, f32[96,512]{1,0:T(8,128)S(1)}, f32[96,512]{1,0:T(8,128)S(1)}, f32[96,512]{1,0:T(8,128)S(1)}, f32[96,512]{1,0:T(8,128)S(1)}, /*index=5*/f32[96,512]{1,0:T(8,128)S(1)}) fusion(f32[384,512]{1,0:T(8,128)} %m.3, s32[]{:T(128)S(6)} %select_n.7, s32[]{:T(128)S(6)} %select_n.6), kind=kLoop, calls=%fused_computation.1 | loop fusion | bytes 2359304 | tf_op jit(solution)/shard_map/dynamic_slice | solution.py:367
  2.4 0.1 collective-permute-start
  2.5 2.4 %collective-permute-start.4 = (f32[96,512]{1,0:T(8,128)S(1)}, f32[96,512]{1,0:T(8,128)S(1)}, u32[]{:S(2)}, u32[]{:S(2)}) collective-permute-start(f32[96,512]{1,0:T(8,128)S(1)} %get-tuple-element.119), channel_id=1, source_target_pairs={{0,255},{1,2},{2,1},{3,4},{4,3},{5,6},{6,5},{7,8},{8,7},{9,10},{10... | collective-permute-start | bytes 589832 | tf_op jit(solution)/shard_map/ppermute | solution.py:348
  4.9 3.2 %collective-permute-start.3 = (f32[96,512]{1,0:T(8,128)S(1)}, f32[96,512]{1,0:T(8,128)S(1)}, u32[]{:S(2)}, u32[]{:S(2)}) collective-permute-start(f32[96,512]{1,0:T(8,128)S(1)} %get-tuple-element.120), channel_id=1, source_target_pairs={{0,128},{1,129},{2,130},{3,131},{4,132},{5,133},{6,134},{7,135},{8... | collective-permute-start | bytes 589832 | tf_op jit(solution)/shard_map/ppermute | solution.py:343
  8.1 6.3 %collective-permute-start.2 = (f32[96,512]{1,0:T(8,128)S(1)}, f32[96,512]{1,0:T(8,128)S(1)}, u32[]{:S(2)}, u32[]{:S(2)}) collective-permute-start(f32[96,512]{1,0:T(8,128)S(1)} %get-tuple-element.121), channel_id=1, source_target_pairs={{0,32},{1,33},{2,34},{3,35},{4,36},{5,37},{6,38},{7,39},{8,40},{9,... | collective-permute-start | bytes 589832 | tf_op jit(solution)/shard_map/ppermute | solution.py:343
  14.4 0.4 collective-permute-start.1
  15.4 0.0 collective-permute-done.core_in
  15.5 0.0 copy-start.2
  15.5 0.0 copy-start.3
  15.5 7.1 %shard_map.146 = (f32[1536,512]{1,0:T(8,128)S(1)}, f32[1536,512]{1,0:T(8,128)S(1)}, f32[384,512]{1,0:T(8,128)S(1)}, bf16[576,1536]{1,0:T(8,128)(2,1)S(1)}, bf16[...) custom-call(s32[1]{0:T(128)} %bitcast.me, ...), custom_call_target="tpu_custom_call" | custom-call | flops 4000000000 | bytes 1048576 | tf_op jit(solution)/shard_map/pallas_call | solution.py:373
  22.6 10.4 %shard_map.147 = (f32[384,512]{1,0:T(8,128)}, f32[384,512]{1,0:T(8,128)S(1)}, f32[96,512]{1,0:T(8,128)S(1)}, f32[96,512]{1,0:T(8,128)S(1)}, f32[96,512]{1,0:T(8,...) custom-call(f32[192,512]{1,0:T(8,128)S(1)} %collective-permute-done., ...), custom_call_target="tpu_custom_call" | custom-call | flops 16000000000 | bytes 1048576 | tf_op jit(solution)/shard_map/pallas_call | solution.py:391
  33.0 0.0 collective-permute-start.10
  33.0 3.5 %collective-permute-done.10.got = f32[264,1536]{1,0:T(8,128)S(1)} collective-permute-done((f32[264,1536]{1,0:T(8,128)S(1)}, f32[264,1536]{1,0:T(8,128)S(1)}, u32[]{:S(2)}, u32[]{:S(2)}) %collective-permute-start.10) | collective-permute-done | bytes 1622048 | tf_op jit(solution)/shard_map/ppermute | solution.py:343
  36.5 0.2 shard_map.150
  36.7 1.1 %collective-permute-start.11 = (f32[136,384]{1,0:T(8,128)S(1)}, f32[136,384]{1,0:T(8,128)S(1)}, u32[]{:S(2)}, u32[]{:S(2)}) collective-permute-start(f32[136,384]{1,0:T(8,128)S(1)} %get-tuple-element.86.send), channel_id=1, source_target_pairs={{0,2},{1,3},{2,0},{3,1},{4,6},{5,7},{6,4},{7,5},{8,10},{9,11},{10,... | collective-permute-start | bytes 626696 | tf_op jit(solution)/shard_map/ppermute | solution.py:343
  37.8 2.7 %collective-permute-start.13 = (f32[136,384]{1,0:T(8,128)S(1)}, f32[136,384]{1,0:T(8,128)S(1)}, u32[]{:S(2)}, u32[]{:S(2)}) collective-permute-start(f32[136,384]{1,0:T(8,128)S(1)} %get-tuple-element.90.send), channel_id=1, source_target_pairs={{0,6},{1,7},{2,4},{3,5},{4,2},{5,3},{6,0},{7,1},{8,14},{9,15},{10,... | collective-permute-start | bytes 626696 | tf_op jit(solution)/shard_map/ppermute | solution.py:343
  40.5 0.7 collective-permute-start.17
  41.2 0.4 collective-permute-start.19
  41.6 2.4 %collective-permute-done.11.got = f32[136,384]{1,0:T(8,128)S(1)} collective-permute-done((f32[136,384]{1,0:T(8,128)S(1)}, f32[136,384]{1,0:T(8,128)S(1)}, u32[]{:S(2)}, u32[]{:S(2)}) %collective-permute-start.11) | collective-permute-done | bytes 208928 | tf_op jit(solution)/shard_map/ppermute | solution.py:343
  44.0 2.4 %collective-permute-start.12 = (f32[72,384]{1,0:T(8,128)S(1)}, f32[72,384]{1,0:T(8,128)S(1)}, u32[]{:S(2)}, u32[]{:S(2)}) collective-permute-start(f32[72,384]{1,0:T(8,128)S(1)} %get-tuple-element.88.send_1), channel_id=1, source_target_pairs={{0,6},{1,7},{2,4},{3,5},{4,2},{5,3},{6,0},{7,1},{8,14},{9,15},{10,... | collective-permute-start | bytes 331784 | tf_op jit(solution)/shard_map/ppermute | solution.py:343
  46.4 0.9 collective-permute-start.14
  47.4 1.1 %collective-permute-start.18 = (f32[72,384]{1,0:T(8,128)S(1)}, f32[72,384]{1,0:T(8,128)S(1)}, u32[]{:S(2)}, u32[]{:S(2)}) collective-permute-start(f32[72,384]{1,0:T(8,128)S(1)} %get-tuple-element.100.send_1), channel_id=1, source_target_pairs={{0,192},{1,193},{2,194},{3,195},{4,196},{5,197},{6,198},{7,199},{8... | collective-permute-start | bytes 331784 | tf_op jit(solution)/shard_map/ppermute | solution.py:343
  48.5 0.2 collective-permute-done.19.got
  48.8 0.2 collective-permute-start.20
  49.0 1.0 collective-permute-done.12.got_1
  50.0 1.2 %collective-permute-done.14.got_2 = f32[72,384]{1,0:T(8,128)S(1)} collective-permute-done((f32[72,384]{1,0:T(8,128)S(1)}, f32[72,384]{1,0:T(8,128)S(1)}, u32[]{:S(2)}, u32[]{:S(2)}) %collective-permute-start.14) | collective-permute-done | bytes 110624 | tf_op jit(solution)/shard_map/ppermute | solution.py:343
  51.3 0.8 collective-permute-start.15
  52.1 1.3 %collective-permute-done.18.got_1 = f32[72,384]{1,0:T(8,128)S(1)} collective-permute-done((f32[72,384]{1,0:T(8,128)S(1)}, f32[72,384]{1,0:T(8,128)S(1)}, u32[]{:S(2)}, u32[]{:S(2)}) %collective-permute-start.18) | collective-permute-done | bytes 110624 | tf_op jit(solution)/shard_map/ppermute | solution.py:343
  53.4 1.2 %collective-permute-done.20.got_2 = f32[72,384]{1,0:T(8,128)S(1)} collective-permute-done((f32[72,384]{1,0:T(8,128)S(1)}, f32[72,384]{1,0:T(8,128)S(1)}, u32[]{:S(2)}, u32[]{:S(2)}) %collective-permute-start.20) | collective-permute-done | bytes 110624 | tf_op jit(solution)/shard_map/ppermute | solution.py:343
  54.7 0.7 collective-permute-start.21
  55.4 0.9 collective-permute-done.15.got
  56.3 1.3 %collective-permute-start.16 = (f32[24,768]{1,0:T(8,128)S(1)}, f32[24,768]{1,0:T(8,128)S(1)}, u32[]{:S(2)}, u32[]{:S(2)}) collective-permute-start(f32[24,768]{1,0:T(8,128)S(1)} %get-tuple-element.96.send_a), channel_id=1, source_target_pairs={{0,192},{1,193},{2,194},{3,195},{4,196},{5,197},{6,198},{7,199},{8... | collective-permute-start | bytes 221192 | tf_op jit(solution)/shard_map/ppermute | solution.py:343
  57.6 2.0 %collective-permute-done.21.got = f32[40,768]{1,0:T(8,128)S(1)} collective-permute-done((f32[40,768]{1,0:T(8,128)S(1)}, f32[40,768]{1,0:T(8,128)S(1)}, u32[]{:S(2)}, u32[]{:S(2)}) %collective-permute-start.21) | collective-permute-done | bytes 122912 | tf_op jit(solution)/shard_map/ppermute | solution.py:343
  59.6 0.8 collective-permute-start.22
  60.4 2.0 %shard_map.148 = (f32[384,512]{1,0:T(8,128)S(1)}, f32[192,512]{1,0:T(8,128)S(1)}, f32[96,512]{1,0:T(8,128)S(1)}) custom-call(bf16[576,1536]{1,0:T(8,128)(2,1)S(1)} %get-tuple-element.72.ot, bf16[1536,512]{1,0:T(8,128)(2,1)S(1)} %get-tuple-element.73.wt_hi, bf16[1536,512]{1,0:T(8,128)(2,1)S(1)} %get-tuple-element.74.wt_lo, ...), custom_call_target="tpu_custom_call" | custom-call | flops 1000000000 | bytes 1048576 | tf_op jit(solution)/shard_map/pallas_call | solution.py:410
  62.4 0.1 collective-permute-start.5
  62.5 2.8 %collective-permute-done.22.got_b = f32[24,768]{1,0:T(8,128)S(1)} collective-permute-done((f32[24,768]{1,0:T(8,128)S(1)}, f32[24,768]{1,0:T(8,128)S(1)}, u32[]{:S(2)}, u32[]{:S(2)}) %collective-permute-start.22) | collective-permute-done | bytes 73760 | tf_op jit(solution)/shard_map/ppermute | solution.py:343
  65.3 3.5 %collective-permute-start.23 = (f32[8,2560]{1,0:T(8,128)S(1)}, f32[8,2560]{1,0:T(8,128)S(1)}, u32[]{:S(2)}, u32[]{:S(2)}) collective-permute-start(f32[8,2560]{1,0:T(8,128)S(1)} %get-tuple-element.110.send), channel_id=1, source_target_pairs={{0,8},{1,9},{2,10},{3,11},{4,12},{5,13},{6,14},{7,15},{8,0},{9,1},... | collective-permute-start | bytes 245768 | tf_op jit(solution)/shard_map/ppermute | solution.py:343
  68.8 2.4 %collective-permute-done.23.got = f32[8,2560]{1,0:T(8,128)S(1)} collective-permute-done((f32[8,2560]{1,0:T(8,128)S(1)}, f32[8,2560]{1,0:T(8,128)S(1)}, u32[]{:S(2)}, u32[]{:S(2)}) %collective-permute-start.23) | collective-permute-done | bytes 81952 | tf_op jit(solution)/shard_map/ppermute | solution.py:343
  71.3 5.2 %collective-permute-start.24 = (f32[8,1792]{1,0:T(8,128)S(1)}, f32[8,1792]{1,0:T(8,128)S(1)}, u32[]{:S(2)}, u32[]{:S(2)}) collective-permute-start(f32[8,1792]{1,0:T(8,128)S(1)} %get-tuple-element.112.send), channel_id=1, source_target_pairs={{0,16},{1,17},{2,18},{3,19},{4,20},{5,21},{6,22},{7,23},{8,24},{9,... | collective-permute-start | bytes 172040 | tf_op jit(solution)/shard_map/ppermute | solution.py:343
  76.5 1.6 %collective-permute-start.6 = (f32[96,512]{1,0:T(8,128)S(1)}, f32[96,512]{1,0:T(8,128)S(1)}, u32[]{:S(2)}, u32[]{:S(2)}) collective-permute-start(f32[96,512]{1,0:T(8,128)S(1)} %get-tuple-element.79), channel_id=1, source_target_pairs={{0,4},{1,5},{2,6},{3,7},{4,0},{5,1},{6,2},{7,3},{8,12},{9,13},{10,... | collective-permute-start | bytes 589832 | tf_op jit(solution)/shard_map/ppermute | solution.py:343
  78.0 5.2 %collective-permute-start.7 = (f32[96,512]{1,0:T(8,128)S(1)}, f32[96,512]{1,0:T(8,128)S(1)}, u32[]{:S(2)}, u32[]{:S(2)}) collective-permute-start(f32[96,512]{1,0:T(8,128)S(1)} %get-tuple-element.80), channel_id=1, source_target_pairs={{0,32},{1,33},{2,34},{3,35},{4,36},{5,37},{6,38},{7,39},{8,40},{9,... | collective-permute-start | bytes 589832 | tf_op jit(solution)/shard_map/ppermute | solution.py:343
  83.2 0.6 collective-permute-start.8
  83.8 1.4 %collective-permute-done.9.side_in = f32[96,512]{1,0:T(8,128)S(1)} collective-permute-done((f32[96,512]{1,0:T(8,128)S(1)}, f32[96,512]{1,0:T(8,128)S(1)}, u32[]{:S(2)}, u32[]{:S(2)}) %collective-permute-start.9) | collective-permute-done | bytes 196640 | tf_op jit(solution)/shard_map/ppermute | solution.py:348
  85.2 15.1 %collective-permute-start.25 = (f32[8,1408]{1,0:T(8,128)S(1)}, f32[8,1408]{1,0:T(8,128)S(1)}, u32[]{:S(2)}, u32[]{:S(2)}) collective-permute-start(f32[8,1408]{1,0:T(8,128)S(1)} %get-tuple-element.114.send), channel_id=1, source_target_pairs={{0,48},{1,49},{2,50},{3,51},{4,52},{5,53},{6,54},{7,55},{8,56},{9,... | collective-permute-start | bytes 135176 | tf_op jit(solution)/shard_map/ppermute | solution.py:343
  100.4 1.0 shard_map.149
  101.4 1.0 collective-permute-done.25.got
  102.4 0.6 shard_map.162
  (43 shorter events, 0.3 us)
Async XLA Ops:
  0.6 14.8 %copy-start = (f32[384,512]{1,0:T(8,128)S(1)}, f32[384,512]{1,0:T(8,128)}, u32[]{:S(2)}) copy-start(f32[384,512]{1,0:T(8,128)} %m.3) | copy-start | bytes 2359300
  0.6 14.8 %copy-start.4 = (f32[16,1536]{1,0:T(8,128)S(1)}, f32[16,1536]{1,0:T(8,128)}, u32[]{:S(2)}) copy-start(f32[16,1536]{1,0:T(8,128)} %coeffs.3) | copy-start | bytes 294916
  0.7 14.8 %copy-start.1 = (f32[2,512,512]{2,1,0:T(8,128)S(1)}, f32[2,512,512]{2,1,0:T(8,128)}, u32[]{:S(2)}) copy-start(f32[2,512,512]{2,1,0:T(8,128)} %wl.1) | copy-start | bytes 6291460
  0.7 14.8 %copy-start.5 = (f32[16,512]{1,0:T(8,128)S(1)}, f32[16,512]{1,0:T(8,128)}, u32[]{:S(2)}) copy-start(f32[16,512]{1,0:T(8,128)} %wb.1) | copy-start | bytes 98308
  0.7 14.8 %copy-start.9 = (s32[12]{0:T(128)S(1)}, s32[12]{0:T(128)}, u32[]{:S(2)}) copy-start(s32[12]{0:T(128)} %blocks.1) | copy-start | bytes 148
  0.7 14.8 %copy-start.7 = (s32[1536]{0:T(1024)S(1)}, s32[1536]{0:T(1024)}, u32[]{:S(2)}) copy-start(s32[1536]{0:T(1024)} %target.1) | copy-start | bytes 18436
  0.7 14.8 %copy-start.6 = (s32[1536]{0:T(1024)S(1)}, s32[1536]{0:T(1024)}, u32[]{:S(2)}) copy-start(s32[1536]{0:T(1024)} %source.1) | copy-start | bytes 18436
  0.7 14.8 %copy-start.8 = (s32[384]{0:T(512)S(1)}, s32[384]{0:T(512)}, u32[]{:S(2)}) copy-start(s32[384]{0:T(512)} %rev.1) | copy-start | bytes 4612
  2.4 13.0 %collective-permute-start = (f32[192,512]{1,0:T(8,128)S(1)}, f32[192,512]{1,0:T(8,128)S(1)}, u32[]{:S(2)}, u32[]{:S(2)}) collective-permute-start(f32[192,512]{1,0:T(8,128)S(1)} %pad_maximum_fusion), channel_id=1, source_target_pairs={{0,1},{1,0},{2,3},{3,2},{4,5},{5,4},{6,7},{7,6},{8,9},{9,8},{10,11... | collective-permute-start | bytes 1179656 | tf_op jit(solution)/shard_map/ppermute | solution.py:343
  2.5 12.9 %collective-permute-start.4 = (f32[96,512]{1,0:T(8,128)S(1)}, f32[96,512]{1,0:T(8,128)S(1)}, u32[]{:S(2)}, u32[]{:S(2)}) collective-permute-start(f32[96,512]{1,0:T(8,128)S(1)} %get-tuple-element.119), channel_id=1, source_target_pairs={{0,255},{1,2},{2,1},{3,4},{4,3},{5,6},{6,5},{7,8},{8,7},{9,10},{10... | collective-permute-start | bytes 589832 | tf_op jit(solution)/shard_map/ppermute | solution.py:348
  4.9 17.7 %collective-permute-start.3 = (f32[96,512]{1,0:T(8,128)S(1)}, f32[96,512]{1,0:T(8,128)S(1)}, u32[]{:S(2)}, u32[]{:S(2)}) collective-permute-start(f32[96,512]{1,0:T(8,128)S(1)} %get-tuple-element.120), channel_id=1, source_target_pairs={{0,128},{1,129},{2,130},{3,131},{4,132},{5,133},{6,134},{7,135},{8... | collective-permute-start | bytes 589832 | tf_op jit(solution)/shard_map/ppermute | solution.py:343
  8.1 14.5 %collective-permute-start.2 = (f32[96,512]{1,0:T(8,128)S(1)}, f32[96,512]{1,0:T(8,128)S(1)}, u32[]{:S(2)}, u32[]{:S(2)}) collective-permute-start(f32[96,512]{1,0:T(8,128)S(1)} %get-tuple-element.121), channel_id=1, source_target_pairs={{0,32},{1,33},{2,34},{3,35},{4,36},{5,37},{6,38},{7,39},{8,40},{9,... | collective-permute-start | bytes 589832 | tf_op jit(solution)/shard_map/ppermute | solution.py:343
  14.4 8.3 %collective-permute-start.1 = (f32[96,512]{1,0:T(8,128)S(1)}, f32[96,512]{1,0:T(8,128)S(1)}, u32[]{:S(2)}, u32[]{:S(2)}) collective-permute-start(f32[96,512]{1,0:T(8,128)S(1)} %get-tuple-element.122), channel_id=1, source_target_pairs={{0,4},{1,5},{2,6},{3,7},{4,0},{5,1},{6,2},{7,3},{8,12},{9,13},{10,... | collective-permute-start | bytes 589832 | tf_op jit(solution)/shard_map/ppermute | solution.py:343
  15.5 7.2 %copy-start.2 = (f32[512,512]{1,0:T(8,128)S(1)}, f32[512,512]{1,0:T(8,128)}, u32[]{:S(2)}) copy-start(f32[512,512]{1,0:T(8,128)} %wr.1) | copy-start | bytes 3145732
  15.5 7.2 %copy-start.3 = (f32[384,512]{1,0:T(8,128)S(1)}, f32[384,512]{1,0:T(8,128)}, u32[]{:S(2)}) copy-start(f32[384,512]{1,0:T(8,128)} %cot.1) | copy-start | bytes 2359300
  33.0 3.5 %collective-permute-start.10 = (f32[264,1536]{1,0:T(8,128)S(1)}, f32[264,1536]{1,0:T(8,128)S(1)}, u32[]{:S(2)}, u32[]{:S(2)}) collective-permute-start(f32[264,1536]{1,0:T(8,128)S(1)} %get-tuple-element.84), channel_id=1, source_target_pairs={{0,1},{1,0},{2,3},{3,2},{4,5},{5,4},{6,7},{7,6},{8,9},{9,8},{10,11... | collective-permute-start | bytes 4866056 | tf_op jit(solution)/shard_map/ppermute | solution.py:343
  36.7 7.3 %collective-permute-start.11 = (f32[136,384]{1,0:T(8,128)S(1)}, f32[136,384]{1,0:T(8,128)S(1)}, u32[]{:S(2)}, u32[]{:S(2)}) collective-permute-start(f32[136,384]{1,0:T(8,128)S(1)} %get-tuple-element.86.send), channel_id=1, source_target_pairs={{0,2},{1,3},{2,0},{3,1},{4,6},{5,7},{6,4},{7,5},{8,10},{9,11},{10,... | collective-permute-start | bytes 626696 | tf_op jit(solution)/shard_map/ppermute | solution.py:343
  37.8 8.6 %collective-permute-start.13 = (f32[136,384]{1,0:T(8,128)S(1)}, f32[136,384]{1,0:T(8,128)S(1)}, u32[]{:S(2)}, u32[]{:S(2)}) collective-permute-start(f32[136,384]{1,0:T(8,128)S(1)} %get-tuple-element.90.send), channel_id=1, source_target_pairs={{0,6},{1,7},{2,4},{3,5},{4,2},{5,3},{6,0},{7,1},{8,14},{9,15},{10,... | collective-permute-start | bytes 626696 | tf_op jit(solution)/shard_map/ppermute | solution.py:343
  40.5 6.8 %collective-permute-start.17 = (f32[136,384]{1,0:T(8,128)S(1)}, f32[136,384]{1,0:T(8,128)S(1)}, u32[]{:S(2)}, u32[]{:S(2)}) collective-permute-start(f32[136,384]{1,0:T(8,128)S(1)} %get-tuple-element.98.send), channel_id=1, source_target_pairs={{0,64},{1,65},{2,66},{3,67},{4,68},{5,69},{6,70},{7,71},{8,72},{9,... | collective-permute-start | bytes 626696 | tf_op jit(solution)/shard_map/ppermute | solution.py:343
  41.2 7.6 %collective-permute-start.19 = (f32[136,384]{1,0:T(8,128)S(1)}, f32[136,384]{1,0:T(8,128)S(1)}, u32[]{:S(2)}, u32[]{:S(2)}) collective-permute-start(f32[136,384]{1,0:T(8,128)S(1)} %get-tuple-element.102.send), channel_id=1, source_target_pairs={{0,192},{1,193},{2,194},{3,195},{4,196},{5,197},{6,198},{7,199},{8... | collective-permute-start | bytes 626696 | tf_op jit(solution)/shard_map/ppermute | solution.py:343
  44.0 6.0 %collective-permute-start.12 = (f32[72,384]{1,0:T(8,128)S(1)}, f32[72,384]{1,0:T(8,128)S(1)}, u32[]{:S(2)}, u32[]{:S(2)}) collective-permute-start(f32[72,384]{1,0:T(8,128)S(1)} %get-tuple-element.88.send_1), channel_id=1, source_target_pairs={{0,6},{1,7},{2,4},{3,5},{4,2},{5,3},{6,0},{7,1},{8,14},{9,15},{10,... | collective-permute-start | bytes 331784 | tf_op jit(solution)/shard_map/ppermute | solution.py:343
  46.4 4.8 %collective-permute-start.14 = (f32[72,384]{1,0:T(8,128)S(1)}, f32[72,384]{1,0:T(8,128)S(1)}, u32[]{:S(2)}, u32[]{:S(2)}) collective-permute-start(f32[72,384]{1,0:T(8,128)S(1)} %get-tuple-element.92.send_2), channel_id=1, source_target_pairs={{0,2},{1,3},{2,0},{3,1},{4,6},{5,7},{6,4},{7,5},{8,10},{9,11},{10,... | collective-permute-start | bytes 331784 | tf_op jit(solution)/shard_map/ppermute | solution.py:343
  47.4 6.0 %collective-permute-start.18 = (f32[72,384]{1,0:T(8,128)S(1)}, f32[72,384]{1,0:T(8,128)S(1)}, u32[]{:S(2)}, u32[]{:S(2)}) collective-permute-start(f32[72,384]{1,0:T(8,128)S(1)} %get-tuple-element.100.send_1), channel_id=1, source_target_pairs={{0,192},{1,193},{2,194},{3,195},{4,196},{5,197},{6,198},{7,199},{8... | collective-permute-start | bytes 331784 | tf_op jit(solution)/shard_map/ppermute | solution.py:343
  48.8 5.8 %collective-permute-start.20 = (f32[72,384]{1,0:T(8,128)S(1)}, f32[72,384]{1,0:T(8,128)S(1)}, u32[]{:S(2)}, u32[]{:S(2)}) collective-permute-start(f32[72,384]{1,0:T(8,128)S(1)} %get-tuple-element.104.send_2), channel_id=1, source_target_pairs={{0,64},{1,65},{2,66},{3,67},{4,68},{5,69},{6,70},{7,71},{8,72},{9,... | collective-permute-start | bytes 331784 | tf_op jit(solution)/shard_map/ppermute | solution.py:343
  51.3 5.0 %collective-permute-start.15 = (f32[40,768]{1,0:T(8,128)S(1)}, f32[40,768]{1,0:T(8,128)S(1)}, u32[]{:S(2)}, u32[]{:S(2)}) collective-permute-start(f32[40,768]{1,0:T(8,128)S(1)} %get-tuple-element.94.send), channel_id=1, source_target_pairs={{0,64},{1,65},{2,66},{3,67},{4,68},{5,69},{6,70},{7,71},{8,72},{9,... | collective-permute-start | bytes 368648 | tf_op jit(solution)/shard_map/ppermute | solution.py:343
  54.7 5.0 %collective-permute-start.21 = (f32[40,768]{1,0:T(8,128)S(1)}, f32[40,768]{1,0:T(8,128)S(1)}, u32[]{:S(2)}, u32[]{:S(2)}) collective-permute-start(f32[40,768]{1,0:T(8,128)S(1)} %get-tuple-element.106.send), channel_id=1, source_target_pairs={{0,2},{1,3},{2,0},{3,1},{4,6},{5,7},{6,4},{7,5},{8,10},{9,11},{10,... | collective-permute-start | bytes 368648 | tf_op jit(solution)/shard_map/ppermute | solution.py:343
  56.3 6.2 %collective-permute-start.16 = (f32[24,768]{1,0:T(8,128)S(1)}, f32[24,768]{1,0:T(8,128)S(1)}, u32[]{:S(2)}, u32[]{:S(2)}) collective-permute-start(f32[24,768]{1,0:T(8,128)S(1)} %get-tuple-element.96.send_a), channel_id=1, source_target_pairs={{0,192},{1,193},{2,194},{3,195},{4,196},{5,197},{6,198},{7,199},{8... | collective-permute-start | bytes 221192 | tf_op jit(solution)/shard_map/ppermute | solution.py:343
  59.6 5.7 %collective-permute-start.22 = (f32[24,768]{1,0:T(8,128)S(1)}, f32[24,768]{1,0:T(8,128)S(1)}, u32[]{:S(2)}, u32[]{:S(2)}) collective-permute-start(f32[24,768]{1,0:T(8,128)S(1)} %get-tuple-element.108.send_b), channel_id=1, source_target_pairs={{0,6},{1,7},{2,4},{3,5},{4,2},{5,3},{6,0},{7,1},{8,14},{9,15},{10,... | collective-permute-start | bytes 221192 | tf_op jit(solution)/shard_map/ppermute | solution.py:343
  62.4 37.9 %collective-permute-start.5 = (f32[192,512]{1,0:T(8,128)S(1)}, f32[192,512]{1,0:T(8,128)S(1)}, u32[]{:S(2)}, u32[]{:S(2)}) collective-permute-start(f32[192,512]{1,0:T(8,128)S(1)} %get-tuple-element.78), channel_id=1, source_target_pairs={{0,1},{1,0},{2,3},{3,2},{4,5},{5,4},{6,7},{7,6},{8,9},{9,8},{10,11... | collective-permute-start | bytes 1179656 | tf_op jit(solution)/shard_map/ppermute | solution.py:343
  65.3 6.0 %collective-permute-start.23 = (f32[8,2560]{1,0:T(8,128)S(1)}, f32[8,2560]{1,0:T(8,128)S(1)}, u32[]{:S(2)}, u32[]{:S(2)}) collective-permute-start(f32[8,2560]{1,0:T(8,128)S(1)} %get-tuple-element.110.send), channel_id=1, source_target_pairs={{0,8},{1,9},{2,10},{3,11},{4,12},{5,13},{6,14},{7,15},{8,0},{9,1},... | collective-permute-start | bytes 245768 | tf_op jit(solution)/shard_map/ppermute | solution.py:343
  71.3 11.9 %collective-permute-start.24 = (f32[8,1792]{1,0:T(8,128)S(1)}, f32[8,1792]{1,0:T(8,128)S(1)}, u32[]{:S(2)}, u32[]{:S(2)}) collective-permute-start(f32[8,1792]{1,0:T(8,128)S(1)} %get-tuple-element.112.send), channel_id=1, source_target_pairs={{0,16},{1,17},{2,18},{3,19},{4,20},{5,21},{6,22},{7,23},{8,24},{9,... | collective-permute-start | bytes 172040 | tf_op jit(solution)/shard_map/ppermute | solution.py:343
  76.5 8.8 %collective-permute-start.9 = (f32[96,512]{1,0:T(8,128)S(1)}, f32[96,512]{1,0:T(8,128)S(1)}, u32[]{:S(2)}, u32[]{:S(2)}) collective-permute-start(f32[96,512]{1,0:T(8,128)S(1)} %get-tuple-element.82), channel_id=1, source_target_pairs={{0,255},{1,2},{2,1},{3,4},{4,3},{5,6},{6,5},{7,8},{8,7},{9,10},{10... | collective-permute-start | bytes 589832 | tf_op jit(solution)/shard_map/ppermute | solution.py:348
  76.5 23.9 %collective-permute-start.6 = (f32[96,512]{1,0:T(8,128)S(1)}, f32[96,512]{1,0:T(8,128)S(1)}, u32[]{:S(2)}, u32[]{:S(2)}) collective-permute-start(f32[96,512]{1,0:T(8,128)S(1)} %get-tuple-element.79), channel_id=1, source_target_pairs={{0,4},{1,5},{2,6},{3,7},{4,0},{5,1},{6,2},{7,3},{8,12},{9,13},{10,... | collective-permute-start | bytes 589832 | tf_op jit(solution)/shard_map/ppermute | solution.py:343
  78.0 22.3 %collective-permute-start.7 = (f32[96,512]{1,0:T(8,128)S(1)}, f32[96,512]{1,0:T(8,128)S(1)}, u32[]{:S(2)}, u32[]{:S(2)}) collective-permute-start(f32[96,512]{1,0:T(8,128)S(1)} %get-tuple-element.80), channel_id=1, source_target_pairs={{0,32},{1,33},{2,34},{3,35},{4,36},{5,37},{6,38},{7,39},{8,40},{9,... | collective-permute-start | bytes 589832 | tf_op jit(solution)/shard_map/ppermute | solution.py:343
  83.2 17.1 %collective-permute-start.8 = (f32[96,512]{1,0:T(8,128)S(1)}, f32[96,512]{1,0:T(8,128)S(1)}, u32[]{:S(2)}, u32[]{:S(2)}) collective-permute-start(f32[96,512]{1,0:T(8,128)S(1)} %get-tuple-element.81), channel_id=1, source_target_pairs={{0,128},{1,129},{2,130},{3,131},{4,132},{5,133},{6,134},{7,135},{8... | collective-permute-start | bytes 589832 | tf_op jit(solution)/shard_map/ppermute | solution.py:343
  85.2 17.1 %collective-permute-start.25 = (f32[8,1408]{1,0:T(8,128)S(1)}, f32[8,1408]{1,0:T(8,128)S(1)}, u32[]{:S(2)}, u32[]{:S(2)}) collective-permute-start(f32[8,1408]{1,0:T(8,128)S(1)} %get-tuple-element.114.send), channel_id=1, source_target_pairs={{0,48},{1,49},{2,50},{3,51},{4,52},{5,53},{6,54},{7,55},{8,56},{9,... | collective-permute-start | bytes 135176 | tf_op jit(solution)/shard_map/ppermute | solution.py:343

commit v3 on v2

--- a/solution.py
+++ b/solution.py
@@ -150,9 +150,9 @@
 
 
 def middle(
-    core_in, a1, a2, a3, m, cot, gath, tw, agg, t2, r, rt, pick, coeffs, wr, wl_hi, wl_lo,
-    out, gmp, gr0, gr1, gr2, gr3, wt_hi, wt_lo, own, send,
-    wr_hi, wr_lo, g2, p, c_s, hs, gp_hi, gp_lo, left,
+    core_in, a1, a2, a3, m, cot, gath, tw, agg, t2, r, pick, coeffs, wr, wl_hi, wl_lo,
+    out, gmp, gr_hi, gr_lo, wr_hi, wr_lo, wt_hi, wt_lo, own, send,
+    g2, p, c_s, hs, gp_hi, gp_lo, left,
 ):
     scale = float(98304) ** -0.5
     arrived = jnp.concatenate([core_in[:HALO, :], a1[...], a2[...], a3[...]], axis=0)
@@ -204,10 +204,7 @@
     gmp[...] = g * (1.0 + gate)
     high, low = split(g * m[...] * slope(rp, rs))
     gp_hi[2, :E], gp_hi[2, E:], gp_lo[2] = high, high, low
-    q = (nn(rt[...], gp_hi[2, :E]).astype(BF16), nn(rt[...], gp_lo[2]).astype(BF16))
-    rows = dot3(nt, q, w_rev)
-    for k, ref in enumerate((gr0, gr1, gr2, gr3)):
-        ref[...] = rows[k * HALO : k * HALO + HALO]
+    gr_hi[...], gr_lo[...] = high, low
     for i in range(SLOTS // CHUNK):
         at = slice(i * CHUNK, (i + 1) * CHUNK)
         prod = nn(t2[at, :], g2[...])
@@ -223,11 +220,15 @@
         ref[256:264, 1024:] = jnp.zeros((8, 512), F32)
 
 
-def scatter(ot, wt_hi, wt_lo, gmp, gr0, gm, core_out, side_out):
+def scatter(ot, wt_hi, wt_lo, gmp, gr_hi, gr_lo, rt, wr_hi, wr_lo, gm, core_out, side_out, gr1, gr2, gr3):
+    q = (nn(rt[...], gr_hi[...]).astype(BF16), nn(rt[...], gr_lo[...]).astype(BF16))
     rims = nn(ot[E:, :], wt_hi[...]) + nn(ot[E:, :], wt_lo[...])
-    core_out[:HALO] = gr0[...]
+    rows = dot3(nt, q, (wr_hi[...], wr_lo[...]))
+    core_out[:HALO] = rows[:HALO]
     core_out[HALO:] = rims[:HALO]
     side_out[...] = rims[HALO:]
+    for k, ref in enumerate((gr1, gr2, gr3)):
+        ref[...] = rows[(k + 1) * HALO : (k + 2) * HALO]
     gm[...] = gmp[...] + (nn(ot[:E, :], wt_hi[...]) + nn(ot[:E, :], wt_lo[...]))
 
 
@@ -388,28 +389,31 @@
         flops=4_000_000_000,
         grant=26,
     )(me, tile_count, tile_block, tri_source, tri_target, rev_slot, tri_basis, w_basis, messages, core_in, side_in, w_layers)
-    out, gmp, gr0, gr1, gr2, gr3, wt_hi, wt_lo, own, send = call(
+    out, gmp, gr_hi, gr_lo, wr_hi, wr_lo, wt_hi, wt_lo, own, send = call(
         middle,
         [
-            ((E, D), F32), ((E, D), F32), quarter, quarter, quarter, quarter,
+            ((E, D), F32), ((E, D), F32), ((E, D), BF16), ((E, D), BF16), ((D, D), BF16), ((D, D), BF16),
             ((SLOTS, D), BF16), ((SLOTS, D), BF16), ((264, 3 * D), F32), ((264, 3 * D), F32),
         ],
-        "v" * 17,
+        "v" * 16,
         [
-            pltpu.VMEM((D, D), BF16), pltpu.VMEM((D, D), BF16),
             pltpu.VMEM((2 * E, D), BF16), pltpu.VMEM((2, SLOTS, D), BF16), pltpu.VMEM((32, SLOTS), BF16),
             pltpu.VMEM((3, 2 * E, D), BF16), pltpu.VMEM((3, 2 * E, D), BF16), pltpu.VMEM((3, E, D), BF16),
             pltpu.VMEM((3, D, 2 * E), BF16),
         ],
         flops=16_000_000_000,
         grant=16,
-    )(core_in, a1, a2, a3, messages, cotangent, gath, tw, agg, t2, r, rt, pick, tri_basis, w_rev, wl_hi, wl_lo)
+    )(core_in, a1, a2, a3, messages, cotangent, gath, tw, agg, t2, r, pick, tri_basis, w_rev, wl_hi, wl_lo)
 
     got = swap(send, 1)
+    gm, core_out, side_out, gr1, gr2, gr3 = call(
+        scatter,
+        [((E, D), F32), ((2 * HALO, D), F32)] + [quarter] * 4,
+        "v" * 9,
+        flops=1_000_000_000,
+        grant=8,
+    )(ot, wt_hi, wt_lo, gmp, gr_hi, gr_lo, rt, wr_hi, wr_lo)
     b2 = swap(gr2, 32)
-    gm, core_out, side_out = call(
-        scatter, [((E, D), F32), ((2 * HALO, D), F32), quarter], "v" * 5, flops=1_000_000_000, grant=6
-    )(ot, wt_hi, wt_lo, gmp, gr0)
     core_back = swap(core_out, 1)
     side_back = swap_side(side_out)
     b1 = swap(gr1, 4)

time: 103 us -> 100 us (0.971)
  the two profiles are of different devices: /device:TPU:64 before, /device:TPU:24 now
where the time goes in v3:
time: 100 us
  starting transfers between devices  44.1 us (44%)
  waiting for transfers between devices  31.6 us (32%)
  Pallas kernels  21.3 us (21%)
  local copies, waits for them, and re-layouts  1.65 us (2%)
  between operations  1.64 us (2%)
    ppermute x24, starting transfers between devices, swap(): return lax.ppermute(value, 'edges', [(i, i ^ mask) for i in range(count)])  28.5 us
    ppermute x24, waiting for transfers between devices, swap(): return lax.ppermute(value, 'edges', [(i, i ^ mask) for i in range(count)])  20.9 us
    ppermute x2, starting transfers between devices, swap_side(): lax.ppermute(value, 'edges', [(i, (i + (1 if i % 2 else -1)) % count) for...  15.6 us
    ppermute x2, waiting for transfers between devices, swap_side(): lax.ppermute(value, 'edges', [(i, (i + (1 if i % 2 else -1)) % count) for...  10.8 us
    pallas_call x1, Pallas kernels, on_device_body(): call(middle, [((E, D), F32), ((E, D), F32), ((E, D), BF16), ((E, D), BF16...  9.15 us
    pallas_call x1, Pallas kernels, on_device_body(): call(prepare, [((SLOTS, D), F32), ((SLOTS, D), F32), ((E, D), F32), ((WIN...  7.1 us
    pallas_call x1, Pallas kernels, on_device_body(): call(scatter, [((E, D), F32), ((2 * HALO, D), F32)] + [quarter] * 4, 'v'...  3.04 us
  transfers between devices with their start and end apart: 26, of which 13 were waited for; matrix products, arithmetic and copies ran while one was open for 0% of the time, Pallas kernels for 11%

profile of v3, /device:TPU:24, one launch (start us, length us, event | category | flops | bytes accessed | tf_op | source)
XLA Modules:
  0.0 100.4 jit_solution(2891599251028168089)
XLA Ops:
  0.7 1.6 %constant_dynamic-slice_fusion = (f32[96,512]{1,0:T(8,128)S(1)}, f32[96,512]{1,0:T(8,128)S(1)}, f32[96,512]{1,0:T(8,128)S(1)}, f32[96,512]{1,0:T(8,128)S(1)}, f32[96,512]{1,0:T(8,128)S(1)}, /*index=5*/f32[96,512]{1,0:T(8,128)S(1)}) fusion(f32[384,512]{1,0:T(8,128)} %m.3, s32[]{:T(128)S(6)} %select_n.7, s32[]{:T(128)S(6)} %select_n.6), kind=kLoop, calls=%fused_computation.1 | loop fusion | bytes 2359304 | tf_op jit(solution)/shard_map/dynamic_slice | solution.py:368
  2.4 0.1 collective-permute-start
  2.5 8.3 %collective-permute-start.4 = (f32[96,512]{1,0:T(8,128)S(1)}, f32[96,512]{1,0:T(8,128)S(1)}, u32[]{:S(2)}, u32[]{:S(2)}) collective-permute-start(f32[96,512]{1,0:T(8,128)S(1)} %get-tuple-element.125), channel_id=1, source_target_pairs={{0,255},{1,2},{2,1},{3,4},{4,3},{5,6},{6,5},{7,8},{8,7},{9,10},{10... | collective-permute-start | bytes 589832 | tf_op jit(solution)/shard_map/ppermute | solution.py:349
  10.8 0.9 collective-permute-start.3
  11.7 1.6 %collective-permute-start.2 = (f32[96,512]{1,0:T(8,128)S(1)}, f32[96,512]{1,0:T(8,128)S(1)}, u32[]{:S(2)}, u32[]{:S(2)}) collective-permute-start(f32[96,512]{1,0:T(8,128)S(1)} %get-tuple-element.127), channel_id=1, source_target_pairs={{0,32},{1,33},{2,34},{3,35},{4,36},{5,37},{6,38},{7,39},{8,40},{9,... | collective-permute-start | bytes 589832 | tf_op jit(solution)/shard_map/ppermute | solution.py:344
  13.3 1.3 %collective-permute-start.1 = (f32[96,512]{1,0:T(8,128)S(1)}, f32[96,512]{1,0:T(8,128)S(1)}, u32[]{:S(2)}, u32[]{:S(2)}) collective-permute-start(f32[96,512]{1,0:T(8,128)S(1)} %get-tuple-element.128), channel_id=1, source_target_pairs={{0,4},{1,5},{2,6},{3,7},{4,0},{5,1},{6,2},{7,3},{8,12},{9,13},{10,... | collective-permute-start | bytes 589832 | tf_op jit(solution)/shard_map/ppermute | solution.py:344
  15.2 7.2 %collective-permute-done.4.side_in = f32[96,512]{1,0:T(8,128)S(1)} collective-permute-done((f32[96,512]{1,0:T(8,128)S(1)}, f32[96,512]{1,0:T(8,128)S(1)}, u32[]{:S(2)}, u32[]{:S(2)}) %collective-permute-start.4) | collective-permute-done | bytes 196640 | tf_op jit(solution)/shard_map/ppermute | solution.py:349
  22.5 0.0 copy-start.2
  22.5 0.0 copy-start.3
  22.5 7.1 %shard_map.146 = (f32[1536,512]{1,0:T(8,128)S(1)}, f32[1536,512]{1,0:T(8,128)S(1)}, f32[384,512]{1,0:T(8,128)S(1)}, bf16[576,1536]{1,0:T(8,128)(2,1)S(1)}, bf16[...) custom-call(s32[1]{0:T(128)} %bitcast.me, ...), custom_call_target="tpu_custom_call" | custom-call | flops 4000000000 | bytes 1048576 | tf_op jit(solution)/shard_map/pallas_call | solution.py:374
  29.7 0.0 collective-permute-done.1.a1
  29.7 9.2 %shard_map.147 = (f32[384,512]{1,0:T(8,128)}, f32[384,512]{1,0:T(8,128)S(1)}, bf16[384,512]{1,0:T(8,128)(2,1)S(1)}, bf16[384,512]{1,0:T(8,128)(2,1)S(1)}, bf16[5...) custom-call(f32[192,512]{1,0:T(8,128)S(1)} %collective-permute-done., ...), custom_call_target="tpu_custom_call" | custom-call | flops 16000000000 | bytes 1048576 | tf_op jit(solution)/shard_map/pallas_call | solution.py:392
  38.8 3.5 %collective-permute-done.10.got = f32[264,1536]{1,0:T(8,128)S(1)} collective-permute-done((f32[264,1536]{1,0:T(8,128)S(1)}, f32[264,1536]{1,0:T(8,128)S(1)}, u32[]{:S(2)}, u32[]{:S(2)}) %collective-permute-start.10) | collective-permute-done | bytes 1622048 | tf_op jit(solution)/shard_map/ppermute | solution.py:344
  42.3 0.2 shard_map.150
  42.5 0.3 collective-permute-start.11
  42.8 0.1 collective-permute-start.13
  42.9 0.5 collective-permute-start.17
  43.4 2.2 %collective-permute-start.19 = (f32[136,384]{1,0:T(8,128)S(1)}, f32[136,384]{1,0:T(8,128)S(1)}, u32[]{:S(2)}, u32[]{:S(2)}) collective-permute-start(f32[136,384]{1,0:T(8,128)S(1)} %get-tuple-element.108.send), channel_id=1, source_target_pairs={{0,192},{1,193},{2,194},{3,195},{4,196},{5,197},{6,198},{7,199},{8... | collective-permute-start | bytes 626696 | tf_op jit(solution)/shard_map/ppermute | solution.py:344
  45.6 4.4 %collective-permute-done.11.got = f32[136,384]{1,0:T(8,128)S(1)} collective-permute-done((f32[136,384]{1,0:T(8,128)S(1)}, f32[136,384]{1,0:T(8,128)S(1)}, u32[]{:S(2)}, u32[]{:S(2)}) %collective-permute-start.11) | collective-permute-done | bytes 208928 | tf_op jit(solution)/shard_map/ppermute | solution.py:344
  50.0 0.1 collective-permute-start.12
  50.1 1.2 %collective-permute-done.13.got = f32[136,384]{1,0:T(8,128)S(1)} collective-permute-done((f32[136,384]{1,0:T(8,128)S(1)}, f32[136,384]{1,0:T(8,128)S(1)}, u32[]{:S(2)}, u32[]{:S(2)}) %collective-permute-start.13) | collective-permute-done | bytes 208928 | tf_op jit(solution)/shard_map/ppermute | solution.py:344
  51.4 0.5 collective-permute-start.14
  51.9 2.5 %collective-permute-start.18 = (f32[72,384]{1,0:T(8,128)S(1)}, f32[72,384]{1,0:T(8,128)S(1)}, u32[]{:S(2)}, u32[]{:S(2)}) collective-permute-start(f32[72,384]{1,0:T(8,128)S(1)} %get-tuple-element.106.send_1), channel_id=1, source_target_pairs={{0,192},{1,193},{2,194},{3,195},{4,196},{5,197},{6,198},{7,199},{8... | collective-permute-start | bytes 331784 | tf_op jit(solution)/shard_map/ppermute | solution.py:344
  54.5 0.1 collective-permute-start.20
  54.6 1.5 %collective-permute-done.12.got_1 = f32[72,384]{1,0:T(8,128)S(1)} collective-permute-done((f32[72,384]{1,0:T(8,128)S(1)}, f32[72,384]{1,0:T(8,128)S(1)}, u32[]{:S(2)}, u32[]{:S(2)}) %collective-permute-start.12) | collective-permute-done | bytes 110624 | tf_op jit(solution)/shard_map/ppermute | solution.py:344
  56.1 0.1 collective-permute-done.14.got_2
  56.2 0.5 collective-permute-start.15
  56.7 1.2 %collective-permute-done.18.got_1 = f32[72,384]{1,0:T(8,128)S(1)} collective-permute-done((f32[72,384]{1,0:T(8,128)S(1)}, f32[72,384]{1,0:T(8,128)S(1)}, u32[]{:S(2)}, u32[]{:S(2)}) %collective-permute-start.18) | collective-permute-done | bytes 110624 | tf_op jit(solution)/shard_map/ppermute | solution.py:344
  58.0 1.6 %collective-permute-done.20.got_2 = f32[72,384]{1,0:T(8,128)S(1)} collective-permute-done((f32[72,384]{1,0:T(8,128)S(1)}, f32[72,384]{1,0:T(8,128)S(1)}, u32[]{:S(2)}, u32[]{:S(2)}) %collective-permute-start.20) | collective-permute-done | bytes 110624 | tf_op jit(solution)/shard_map/ppermute | solution.py:344
  59.6 1.7 %collective-permute-start.21 = (f32[40,768]{1,0:T(8,128)S(1)}, f32[40,768]{1,0:T(8,128)S(1)}, u32[]{:S(2)}, u32[]{:S(2)}) collective-permute-start(f32[40,768]{1,0:T(8,128)S(1)} %get-tuple-element.112.send), channel_id=1, source_target_pairs={{0,2},{1,3},{2,0},{3,1},{4,6},{5,7},{6,4},{7,5},{8,10},{9,11},{10,... | collective-permute-start | bytes 368648 | tf_op jit(solution)/shard_map/ppermute | solution.py:344
  61.3 2.4 %collective-permute-start.16 = (f32[24,768]{1,0:T(8,128)S(1)}, f32[24,768]{1,0:T(8,128)S(1)}, u32[]{:S(2)}, u32[]{:S(2)}) collective-permute-start(f32[24,768]{1,0:T(8,128)S(1)} %get-tuple-element.102.send_a), channel_id=1, source_target_pairs={{0,192},{1,193},{2,194},{3,195},{4,196},{5,197},{6,198},{7,199},{8... | collective-permute-start | bytes 221192 | tf_op jit(solution)/shard_map/ppermute | solution.py:344
  63.8 0.8 collective-permute-done.21.got
  64.6 2.0 %collective-permute-start.22 = (f32[24,768]{1,0:T(8,128)S(1)}, f32[24,768]{1,0:T(8,128)S(1)}, u32[]{:S(2)}, u32[]{:S(2)}) collective-permute-start(f32[24,768]{1,0:T(8,128)S(1)} %get-tuple-element.114.send_b), channel_id=1, source_target_pairs={{0,6},{1,7},{2,4},{3,5},{4,2},{5,3},{6,0},{7,1},{8,14},{9,15},{10,... | collective-permute-start | bytes 221192 | tf_op jit(solution)/shard_map/ppermute | solution.py:344
  66.5 3.0 %shard_map.148 = (f32[384,512]{1,0:T(8,128)S(1)}, f32[192,512]{1,0:T(8,128)S(1)}, f32[96,512]{1,0:T(8,128)S(1)}, f32[96,512]{1,0:T(8,128)S(1)}, f32[96,512]{1,0:T(8,128)S(1)}, /*index=5*/f32[96,512]{1,0:T(8,128)S(1)}) custom-call(bf16[576,1536]{1,0:T(8,128)(2,1)S(1)} %get-tuple-element.74.ot, bf16[1536,512]{1,0:T(8,128)(2,1)S(1)} %get-tuple-element.75.wt_hi, ...), custom_call_target="tpu_custom_call" | custom-call | flops 1000000000 | bytes 1048576 | tf_op jit(solution)/shard_map/pallas_call | solution.py:409
  69.6 0.1 collective-permute-start.5
  69.7 0.5 collective-permute-done.22.got_b
  70.2 0.1 collective-permute-start.23
  70.3 4.4 %collective-permute-done.23.got = f32[8,2560]{1,0:T(8,128)S(1)} collective-permute-done((f32[8,2560]{1,0:T(8,128)S(1)}, f32[8,2560]{1,0:T(8,128)S(1)}, u32[]{:S(2)}, u32[]{:S(2)}) %collective-permute-start.23) | collective-permute-done | bytes 81952 | tf_op jit(solution)/shard_map/ppermute | solution.py:344
  74.8 0.1 collective-permute-start.24
  74.9 1.8 %collective-permute-start.6 = (f32[96,512]{1,0:T(8,128)S(1)}, f32[96,512]{1,0:T(8,128)S(1)}, u32[]{:S(2)}, u32[]{:S(2)}) collective-permute-start(f32[96,512]{1,0:T(8,128)S(1)} %get-tuple-element.85), channel_id=1, source_target_pairs={{0,4},{1,5},{2,6},{3,7},{4,0},{5,1},{6,2},{7,3},{8,12},{9,13},{10,... | collective-permute-start | bytes 589832 | tf_op jit(solution)/shard_map/ppermute | solution.py:344
  76.7 7.2 %collective-permute-start.7 = (f32[96,512]{1,0:T(8,128)S(1)}, f32[96,512]{1,0:T(8,128)S(1)}, u32[]{:S(2)}, u32[]{:S(2)}) collective-permute-start(f32[96,512]{1,0:T(8,128)S(1)} %get-tuple-element.86), channel_id=1, source_target_pairs={{0,32},{1,33},{2,34},{3,35},{4,36},{5,37},{6,38},{7,39},{8,40},{9,... | collective-permute-start | bytes 589832 | tf_op jit(solution)/shard_map/ppermute | solution.py:344
  83.9 2.4 %collective-permute-start.8 = (f32[96,512]{1,0:T(8,128)S(1)}, f32[96,512]{1,0:T(8,128)S(1)}, u32[]{:S(2)}, u32[]{:S(2)}) collective-permute-start(f32[96,512]{1,0:T(8,128)S(1)} %get-tuple-element.87), channel_id=1, source_target_pairs={{0,128},{1,129},{2,130},{3,131},{4,132},{5,133},{6,134},{7,135},{8... | collective-permute-start | bytes 589832 | tf_op jit(solution)/shard_map/ppermute | solution.py:344
  86.2 7.2 %collective-permute-start.9 = (f32[96,512]{1,0:T(8,128)S(1)}, f32[96,512]{1,0:T(8,128)S(1)}, u32[]{:S(2)}, u32[]{:S(2)}) collective-permute-start(f32[96,512]{1,0:T(8,128)S(1)} %get-tuple-element.88), channel_id=1, source_target_pairs={{0,255},{1,2},{2,1},{3,4},{4,3},{5,6},{6,5},{7,8},{8,7},{9,10},{10... | collective-permute-start | bytes 589832 | tf_op jit(solution)/shard_map/ppermute | solution.py:349
  93.5 0.1 collective-permute-start.25
  93.6 3.5 %collective-permute-done.9.side_in = f32[96,512]{1,0:T(8,128)S(1)} collective-permute-done((f32[96,512]{1,0:T(8,128)S(1)}, f32[96,512]{1,0:T(8,128)S(1)}, u32[]{:S(2)}, u32[]{:S(2)}) %collective-permute-start.9) | collective-permute-done | bytes 196640 | tf_op jit(solution)/shard_map/ppermute | solution.py:349
  97.2 1.0 %shard_map.149 = f32[384,512]{1,0:T(8,128)} custom-call(s32[1]{0:T(128)} %bitcast.me, f32[384,512]{1,0:T(8,128)S(1)} %get-tuple-element.83.gm, f32[192,512]{1,0:T(8,128)S(1)} %collective-permute-done.5.core_in, f32[96,512]{1,0:T(8,128)S(1)} %collective-permute-done.6.g1, f32[96,512]{1,0:T(8,128)S(1)} %collective-permute-done.7.g2, ...), custom_call_target="tpu_custom_call" | custom-call | flops 1000000 | bytes 1048576 | tf_op jit(solution)/shard_map/pallas_call | solution.py:421
  98.2 1.6 %collective-permute-done.25.got = f32[8,1408]{1,0:T(8,128)S(1)} collective-permute-done((f32[8,1408]{1,0:T(8,128)S(1)}, f32[8,1408]{1,0:T(8,128)S(1)}, u32[]{:S(2)}, u32[]{:S(2)}) %collective-permute-start.25) | collective-permute-done | bytes 45088 | tf_op jit(solution)/shard_map/ppermute | solution.py:344
  99.8 0.6 shard_map.162
  (43 shorter events, 0.3 us)
Async XLA Ops:
  0.6 21.8 %copy-start = (f32[384,512]{1,0:T(8,128)S(1)}, f32[384,512]{1,0:T(8,128)}, u32[]{:S(2)}) copy-start(f32[384,512]{1,0:T(8,128)} %m.3) | copy-start | bytes 2359300
  0.6 21.8 %copy-start.4 = (f32[16,1536]{1,0:T(8,128)S(1)}, f32[16,1536]{1,0:T(8,128)}, u32[]{:S(2)}) copy-start(f32[16,1536]{1,0:T(8,128)} %coeffs.3) | copy-start | bytes 294916
  0.7 21.8 %copy-start.1 = (f32[2,512,512]{2,1,0:T(8,128)S(1)}, f32[2,512,512]{2,1,0:T(8,128)}, u32[]{:S(2)}) copy-start(f32[2,512,512]{2,1,0:T(8,128)} %wl.1) | copy-start | bytes 6291460
  0.7 21.8 %copy-start.5 = (f32[16,512]{1,0:T(8,128)S(1)}, f32[16,512]{1,0:T(8,128)}, u32[]{:S(2)}) copy-start(f32[16,512]{1,0:T(8,128)} %wb.1) | copy-start | bytes 98308
  0.7 21.8 %copy-start.9 = (s32[12]{0:T(128)S(1)}, s32[12]{0:T(128)}, u32[]{:S(2)}) copy-start(s32[12]{0:T(128)} %blocks.1) | copy-start | bytes 148
  0.7 21.8 %copy-start.7 = (s32[1536]{0:T(1024)S(1)}, s32[1536]{0:T(1024)}, u32[]{:S(2)}) copy-start(s32[1536]{0:T(1024)} %target.1) | copy-start | bytes 18436
  0.7 21.8 %copy-start.6 = (s32[1536]{0:T(1024)S(1)}, s32[1536]{0:T(1024)}, u32[]{:S(2)}) copy-start(s32[1536]{0:T(1024)} %source.1) | copy-start | bytes 18436
  0.7 21.8 %copy-start.8 = (s32[384]{0:T(512)S(1)}, s32[384]{0:T(512)}, u32[]{:S(2)}) copy-start(s32[384]{0:T(512)} %rev.1) | copy-start | bytes 4612
  2.4 20.1 %collective-permute-start = (f32[192,512]{1,0:T(8,128)S(1)}, f32[192,512]{1,0:T(8,128)S(1)}, u32[]{:S(2)}, u32[]{:S(2)}) collective-permute-start(f32[192,512]{1,0:T(8,128)S(1)} %pad_maximum_fusion), channel_id=1, source_target_pairs={{0,1},{1,0},{2,3},{3,2},{4,5},{5,4},{6,7},{7,6},{8,9},{9,8},{10,11... | collective-permute-start | bytes 1179656 | tf_op jit(solution)/shard_map/ppermute | solution.py:344
  2.5 20.0 %collective-permute-start.4 = (f32[96,512]{1,0:T(8,128)S(1)}, f32[96,512]{1,0:T(8,128)S(1)}, u32[]{:S(2)}, u32[]{:S(2)}) collective-permute-start(f32[96,512]{1,0:T(8,128)S(1)} %get-tuple-element.125), channel_id=1, source_target_pairs={{0,255},{1,2},{2,1},{3,4},{4,3},{5,6},{6,5},{7,8},{8,7},{9,10},{10... | collective-permute-start | bytes 589832 | tf_op jit(solution)/shard_map/ppermute | solution.py:349
  10.8 18.8 %collective-permute-start.3 = (f32[96,512]{1,0:T(8,128)S(1)}, f32[96,512]{1,0:T(8,128)S(1)}, u32[]{:S(2)}, u32[]{:S(2)}) collective-permute-start(f32[96,512]{1,0:T(8,128)S(1)} %get-tuple-element.126), channel_id=1, source_target_pairs={{0,128},{1,129},{2,130},{3,131},{4,132},{5,133},{6,134},{7,135},{8... | collective-permute-start | bytes 589832 | tf_op jit(solution)/shard_map/ppermute | solution.py:344
  11.7 17.9 %collective-permute-start.2 = (f32[96,512]{1,0:T(8,128)S(1)}, f32[96,512]{1,0:T(8,128)S(1)}, u32[]{:S(2)}, u32[]{:S(2)}) collective-permute-start(f32[96,512]{1,0:T(8,128)S(1)} %get-tuple-element.127), channel_id=1, source_target_pairs={{0,32},{1,33},{2,34},{3,35},{4,36},{5,37},{6,38},{7,39},{8,40},{9,... | collective-permute-start | bytes 589832 | tf_op jit(solution)/shard_map/ppermute | solution.py:344
  13.3 16.4 %collective-permute-start.1 = (f32[96,512]{1,0:T(8,128)S(1)}, f32[96,512]{1,0:T(8,128)S(1)}, u32[]{:S(2)}, u32[]{:S(2)}) collective-permute-start(f32[96,512]{1,0:T(8,128)S(1)} %get-tuple-element.128), channel_id=1, source_target_pairs={{0,4},{1,5},{2,6},{3,7},{4,0},{5,1},{6,2},{7,3},{8,12},{9,13},{10,... | collective-permute-start | bytes 589832 | tf_op jit(solution)/shard_map/ppermute | solution.py:344
  22.5 7.2 %copy-start.2 = (f32[512,512]{1,0:T(8,128)S(1)}, f32[512,512]{1,0:T(8,128)}, u32[]{:S(2)}) copy-start(f32[512,512]{1,0:T(8,128)} %wr.1) | copy-start | bytes 3145732
  22.5 7.2 %copy-start.3 = (f32[384,512]{1,0:T(8,128)S(1)}, f32[384,512]{1,0:T(8,128)}, u32[]{:S(2)}) copy-start(f32[384,512]{1,0:T(8,128)} %cot.1) | copy-start | bytes 2359300
  38.8 3.5 %collective-permute-start.10 = (f32[264,1536]{1,0:T(8,128)S(1)}, f32[264,1536]{1,0:T(8,128)S(1)}, u32[]{:S(2)}, u32[]{:S(2)}) collective-permute-start(f32[264,1536]{1,0:T(8,128)S(1)} %get-tuple-element.90), channel_id=1, source_target_pairs={{0,1},{1,0},{2,3},{3,2},{4,5},{5,4},{6,7},{7,6},{8,9},{9,8},{10,11... | collective-permute-start | bytes 4866056 | tf_op jit(solution)/shard_map/ppermute | solution.py:344
  42.5 7.5 %collective-permute-start.11 = (f32[136,384]{1,0:T(8,128)S(1)}, f32[136,384]{1,0:T(8,128)S(1)}, u32[]{:S(2)}, u32[]{:S(2)}) collective-permute-start(f32[136,384]{1,0:T(8,128)S(1)} %get-tuple-element.92.send), channel_id=1, source_target_pairs={{0,2},{1,3},{2,0},{3,1},{4,6},{5,7},{6,4},{7,5},{8,10},{9,11},{10,... | collective-permute-start | bytes 626696 | tf_op jit(solution)/shard_map/ppermute | solution.py:344
  42.8 8.5 %collective-permute-start.13 = (f32[136,384]{1,0:T(8,128)S(1)}, f32[136,384]{1,0:T(8,128)S(1)}, u32[]{:S(2)}, u32[]{:S(2)}) collective-permute-start(f32[136,384]{1,0:T(8,128)S(1)} %get-tuple-element.96.send), channel_id=1, source_target_pairs={{0,6},{1,7},{2,4},{3,5},{4,2},{5,3},{6,0},{7,1},{8,14},{9,15},{10,... | collective-permute-start | bytes 626696 | tf_op jit(solution)/shard_map/ppermute | solution.py:344
  42.9 9.0 %collective-permute-start.17 = (f32[136,384]{1,0:T(8,128)S(1)}, f32[136,384]{1,0:T(8,128)S(1)}, u32[]{:S(2)}, u32[]{:S(2)}) collective-permute-start(f32[136,384]{1,0:T(8,128)S(1)} %get-tuple-element.104.send), channel_id=1, source_target_pairs={{0,64},{1,65},{2,66},{3,67},{4,68},{5,69},{6,70},{7,71},{8,72},{9,... | collective-permute-start | bytes 626696 | tf_op jit(solution)/shard_map/ppermute | solution.py:344
  43.4 11.0 %collective-permute-start.19 = (f32[136,384]{1,0:T(8,128)S(1)}, f32[136,384]{1,0:T(8,128)S(1)}, u32[]{:S(2)}, u32[]{:S(2)}) collective-permute-start(f32[136,384]{1,0:T(8,128)S(1)} %get-tuple-element.108.send), channel_id=1, source_target_pairs={{0,192},{1,193},{2,194},{3,195},{4,196},{5,197},{6,198},{7,199},{8... | collective-permute-start | bytes 626696 | tf_op jit(solution)/shard_map/ppermute | solution.py:344
  50.0 6.0 %collective-permute-start.12 = (f32[72,384]{1,0:T(8,128)S(1)}, f32[72,384]{1,0:T(8,128)S(1)}, u32[]{:S(2)}, u32[]{:S(2)}) collective-permute-start(f32[72,384]{1,0:T(8,128)S(1)} %get-tuple-element.94.send_1), channel_id=1, source_target_pairs={{0,6},{1,7},{2,4},{3,5},{4,2},{5,3},{6,0},{7,1},{8,14},{9,15},{10,... | collective-permute-start | bytes 331784 | tf_op jit(solution)/shard_map/ppermute | solution.py:344
  51.4 4.8 %collective-permute-start.14 = (f32[72,384]{1,0:T(8,128)S(1)}, f32[72,384]{1,0:T(8,128)S(1)}, u32[]{:S(2)}, u32[]{:S(2)}) collective-permute-start(f32[72,384]{1,0:T(8,128)S(1)} %get-tuple-element.98.send_2), channel_id=1, source_target_pairs={{0,2},{1,3},{2,0},{3,1},{4,6},{5,7},{6,4},{7,5},{8,10},{9,11},{10,... | collective-permute-start | bytes 331784 | tf_op jit(solution)/shard_map/ppermute | solution.py:344
  51.9 6.0 %collective-permute-start.18 = (f32[72,384]{1,0:T(8,128)S(1)}, f32[72,384]{1,0:T(8,128)S(1)}, u32[]{:S(2)}, u32[]{:S(2)}) collective-permute-start(f32[72,384]{1,0:T(8,128)S(1)} %get-tuple-element.106.send_1), channel_id=1, source_target_pairs={{0,192},{1,193},{2,194},{3,195},{4,196},{5,197},{6,198},{7,199},{8... | collective-permute-start | bytes 331784 | tf_op jit(solution)/shard_map/ppermute | solution.py:344
  54.5 5.0 %collective-permute-start.20 = (f32[72,384]{1,0:T(8,128)S(1)}, f32[72,384]{1,0:T(8,128)S(1)}, u32[]{:S(2)}, u32[]{:S(2)}) collective-permute-start(f32[72,384]{1,0:T(8,128)S(1)} %get-tuple-element.110.send_2), channel_id=1, source_target_pairs={{0,64},{1,65},{2,66},{3,67},{4,68},{5,69},{6,70},{7,71},{8,72},{9,... | collective-permute-start | bytes 331784 | tf_op jit(solution)/shard_map/ppermute | solution.py:344
  56.2 5.1 %collective-permute-start.15 = (f32[40,768]{1,0:T(8,128)S(1)}, f32[40,768]{1,0:T(8,128)S(1)}, u32[]{:S(2)}, u32[]{:S(2)}) collective-permute-start(f32[40,768]{1,0:T(8,128)S(1)} %get-tuple-element.100.send), channel_id=1, source_target_pairs={{0,64},{1,65},{2,66},{3,67},{4,68},{5,69},{6,70},{7,71},{8,72},{9,... | collective-permute-start | bytes 368648 | tf_op jit(solution)/shard_map/ppermute | solution.py:344
  59.6 5.0 %collective-permute-start.21 = (f32[40,768]{1,0:T(8,128)S(1)}, f32[40,768]{1,0:T(8,128)S(1)}, u32[]{:S(2)}, u32[]{:S(2)}) collective-permute-start(f32[40,768]{1,0:T(8,128)S(1)} %get-tuple-element.112.send), channel_id=1, source_target_pairs={{0,2},{1,3},{2,0},{3,1},{4,6},{5,7},{6,4},{7,5},{8,10},{9,11},{10,... | collective-permute-start | bytes 368648 | tf_op jit(solution)/shard_map/ppermute | solution.py:344
  61.3 8.4 %collective-permute-start.16 = (f32[24,768]{1,0:T(8,128)S(1)}, f32[24,768]{1,0:T(8,128)S(1)}, u32[]{:S(2)}, u32[]{:S(2)}) collective-permute-start(f32[24,768]{1,0:T(8,128)S(1)} %get-tuple-element.102.send_a), channel_id=1, source_target_pairs={{0,192},{1,193},{2,194},{3,195},{4,196},{5,197},{6,198},{7,199},{8... | collective-permute-start | bytes 221192 | tf_op jit(solution)/shard_map/ppermute | solution.py:344
  64.6 5.7 %collective-permute-start.22 = (f32[24,768]{1,0:T(8,128)S(1)}, f32[24,768]{1,0:T(8,128)S(1)}, u32[]{:S(2)}, u32[]{:S(2)}) collective-permute-start(f32[24,768]{1,0:T(8,128)S(1)} %get-tuple-element.114.send_b), channel_id=1, source_target_pairs={{0,6},{1,7},{2,4},{3,5},{4,2},{5,3},{6,0},{7,1},{8,14},{9,15},{10,... | collective-permute-start | bytes 221192 | tf_op jit(solution)/shard_map/ppermute | solution.py:344
  69.6 27.6 %collective-permute-start.5 = (f32[192,512]{1,0:T(8,128)S(1)}, f32[192,512]{1,0:T(8,128)S(1)}, u32[]{:S(2)}, u32[]{:S(2)}) collective-permute-start(f32[192,512]{1,0:T(8,128)S(1)} %get-tuple-element.84), channel_id=1, source_target_pairs={{0,1},{1,0},{2,3},{3,2},{4,5},{5,4},{6,7},{7,6},{8,9},{9,8},{10,11... | collective-permute-start | bytes 1179656 | tf_op jit(solution)/shard_map/ppermute | solution.py:344
  70.2 4.5 %collective-permute-start.23 = (f32[8,2560]{1,0:T(8,128)S(1)}, f32[8,2560]{1,0:T(8,128)S(1)}, u32[]{:S(2)}, u32[]{:S(2)}) collective-permute-start(f32[8,2560]{1,0:T(8,128)S(1)} %get-tuple-element.116.send), channel_id=1, source_target_pairs={{0,8},{1,9},{2,10},{3,11},{4,12},{5,13},{6,14},{7,15},{8,0},{9,1},... | collective-permute-start | bytes 245768 | tf_op jit(solution)/shard_map/ppermute | solution.py:344
  74.8 11.5 %collective-permute-start.24 = (f32[8,1792]{1,0:T(8,128)S(1)}, f32[8,1792]{1,0:T(8,128)S(1)}, u32[]{:S(2)}, u32[]{:S(2)}) collective-permute-start(f32[8,1792]{1,0:T(8,128)S(1)} %get-tuple-element.118.send), channel_id=1, source_target_pairs={{0,16},{1,17},{2,18},{3,19},{4,20},{5,21},{6,22},{7,23},{8,24},{9,... | collective-permute-start | bytes 172040 | tf_op jit(solution)/shard_map/ppermute | solution.py:344
  74.9 18.6 %collective-permute-start.6 = (f32[96,512]{1,0:T(8,128)S(1)}, f32[96,512]{1,0:T(8,128)S(1)}, u32[]{:S(2)}, u32[]{:S(2)}) collective-permute-start(f32[96,512]{1,0:T(8,128)S(1)} %get-tuple-element.85), channel_id=1, source_target_pairs={{0,4},{1,5},{2,6},{3,7},{4,0},{5,1},{6,2},{7,3},{8,12},{9,13},{10,... | collective-permute-start | bytes 589832 | tf_op jit(solution)/shard_map/ppermute | solution.py:344
  76.7 16.9 %collective-permute-start.7 = (f32[96,512]{1,0:T(8,128)S(1)}, f32[96,512]{1,0:T(8,128)S(1)}, u32[]{:S(2)}, u32[]{:S(2)}) collective-permute-start(f32[96,512]{1,0:T(8,128)S(1)} %get-tuple-element.86), channel_id=1, source_target_pairs={{0,32},{1,33},{2,34},{3,35},{4,36},{5,37},{6,38},{7,39},{8,40},{9,... | collective-permute-start | bytes 589832 | tf_op jit(solution)/shard_map/ppermute | solution.py:344
  83.9 9.7 %collective-permute-start.8 = (f32[96,512]{1,0:T(8,128)S(1)}, f32[96,512]{1,0:T(8,128)S(1)}, u32[]{:S(2)}, u32[]{:S(2)}) collective-permute-start(f32[96,512]{1,0:T(8,128)S(1)} %get-tuple-element.87), channel_id=1, source_target_pairs={{0,128},{1,129},{2,130},{3,131},{4,132},{5,133},{6,134},{7,135},{8... | collective-permute-start | bytes 589832 | tf_op jit(solution)/shard_map/ppermute | solution.py:344
  86.2 10.9 %collective-permute-start.9 = (f32[96,512]{1,0:T(8,128)S(1)}, f32[96,512]{1,0:T(8,128)S(1)}, u32[]{:S(2)}, u32[]{:S(2)}) collective-permute-start(f32[96,512]{1,0:T(8,128)S(1)} %get-tuple-element.88), channel_id=1, source_target_pairs={{0,255},{1,2},{2,1},{3,4},{4,3},{5,6},{6,5},{7,8},{8,7},{9,10},{10... | collective-permute-start | bytes 589832 | tf_op jit(solution)/shard_map/ppermute | solution.py:349
  93.5 6.2 %collective-permute-start.25 = (f32[8,1408]{1,0:T(8,128)S(1)}, f32[8,1408]{1,0:T(8,128)S(1)}, u32[]{:S(2)}, u32[]{:S(2)}) collective-permute-start(f32[8,1408]{1,0:T(8,128)S(1)} %get-tuple-element.120.send), channel_id=1, source_target_pairs={{0,48},{1,49},{2,50},{3,51},{4,52},{5,53},{6,54},{7,55},{8,56},{9,... | collective-permute-start | bytes 135176 | tf_op jit(solution)/shard_map/ppermute | solution.py:344
